TPU v7x, 128 devices: a whole 4x4x4 slice. The times are simulated.
128 devices in a mesh: band: 4 (over x), tile: 32 (over z, y, core).
Axes of the slice: x: 4, y: 4, z: 4, core: 2. Of those that a mesh axis runs over, the one named last changes fastest.
Arguments:
- obs_values: float32 [2, 32, 262144], P(None, None, ('band', 'tile')), may hold values from -6 to 6
- obs_place: float32 [3, 262144], P(None, ('band', 'tile')), as said below
- obs_depth: int32 [262144], P(('band', 'tile')), may hold values from 0 to 32, as said below
- node_place: float32 [2, 4096], P(None, 'tile'), as said below
- neighbours: int32 [4096, 1024], P('tile'), may hold values from 0 to 24575
- counts: int32 [4096], P('tile'), may hold values from 1 to 1024, as said below
Outputs:
- mapped: float32 [2, 32, 4096], P(None, 'band', 'tile')
Inputs may be any that keep to these rules, and one draw needn't show every extreme that they name: `obs_place`: A profile in bucket j of its device's block (slots j * 64 to (j + 1) * 64 - 1) lies between longitudes -pi + j * 2 pi / 32 and -pi + (j + 1) * 2 pi / 32; latitudes lie within -1 and 1; the day angle within -pi and pi. `obs_depth`: 0 marks an empty slot; the first slot of every bucket holds a profile. `node_place`: the nodes of tile j lie between longitudes -pi + j * 2 pi / 32 and -pi + (j + 1) * 2 pi / 32, at latitudes within -1 and 1. `neighbours`: entries at list positions from counts[n] onward are padding. `counts`: the first node of every tile has a full list.
All inputs are finite; a program needn't handle non-finite values.
Results may differ from a plain program's by a relative error of at most 0.0003.
Values sent between devices are 32-bit elements; how exact they have to be, the bound alone decides.
A program may use at most 128 MiB of HBM per device.

v0:
```python
import math

import jax
import jax.numpy as jnp
from jax import lax
from jax.sharding import PartitionSpec as P

SPREAD = 0.5
RIDGE_WEIGHT = 1.0
MONTH_ANGLE = -11.0 * math.pi / 12.0
BASIS_PAIRS = [
    (first_index, second_index)
    for first_index in range(5)
    for second_index in range(first_index, 5)
]
HIGHEST = lax.Precision.HIGHEST


def padded(block, sides, width):
    for axis, dim in sides:
        count = lax.axis_size(axis)
        forward = [(i, i + 1) for i in range(count - 1)]
        forward.append((count - 1, 0))
        backward = [(target, source) for source, target in forward]
        low = lax.ppermute(
            lax.slice_in_dim(block, block.shape[dim] - width, None, axis=dim), axis, forward
        )
        high = lax.ppermute(lax.slice_in_dim(block, 0, width, axis=dim), axis, backward)
        block = jnp.concatenate([low, block, high], axis=dim)
    return block


def profile_rows(obs_place, obs_depth):
    longitude, latitude, day_angle = (obs_place[0], obs_place[1], obs_place[2])
    cos_lat = jnp.cos(latitude)
    return jnp.stack(
        [
            cos_lat * jnp.cos(longitude),
            cos_lat * jnp.sin(longitude),
            jnp.sin(latitude),
            jnp.cos(day_angle),
            jnp.sin(day_angle),
            obs_depth.astype(jnp.float32),
        ]
    )


def node_frames(longitude, latitude):
    sin_lat, cos_lat = (jnp.sin(latitude), jnp.cos(latitude))
    sin_lon, cos_lon = (jnp.sin(longitude), jnp.cos(longitude))
    return [
        cos_lat * cos_lon,
        cos_lat * sin_lon,
        sin_lat,
        -sin_lon,
        cos_lon,
        -sin_lat * cos_lon,
        -sin_lat * sin_lon,
        cos_lat,
    ]


def block_terms(picked, node_frame, valid_mask, level_ids):
    levels = level_ids.shape[0]
    unit_x, unit_y, unit_z = (picked[2 * levels], picked[2 * levels + 1], picked[2 * levels + 2])
    node_x, node_y, node_z, east_x, east_y, north_x, north_y, north_z = node_frame
    chord_sq = (unit_x - node_x) ** 2 + (unit_y - node_y) ** 2 + (unit_z - node_z) ** 2
    weight = jnp.exp(-chord_sq / (SPREAD * SPREAD)) * valid_mask
    east_off = (unit_x * east_x + unit_y * east_y) / SPREAD
    north_off = (unit_x * north_x + unit_y * north_y + unit_z * north_z) / SPREAD
    basis_rows = [
        jnp.ones_like(weight),
        east_off,
        north_off,
        picked[2 * levels + 3],
        picked[2 * levels + 4],
    ]
    depth_rows = picked[2 * levels + 5]
    inside = (level_ids[:, None, None] < depth_rows[None]).astype(jnp.float32)
    crossed = jnp.stack(
        [
            weight * basis_rows[left_index] * basis_rows[right_index]
            for left_index, right_index in BASIS_PAIRS
        ]
    )
    normal = jnp.einsum("pnk,lnk->pln", crossed, inside, precision=HIGHEST)
    values = (
        picked[: 2 * levels].reshape(2, levels, picked.shape[1], picked.shape[2]) * inside[None]
    )
    weighted = jnp.stack([weight * basis_one for basis_one in basis_rows])
    moments = jnp.einsum("pnk,vlnk->pvln", weighted, values, precision=HIGHEST)
    return (normal, moments)


def solve_fit(normal, moments):
    position = {}
    for place_index, pair in enumerate(BASIS_PAIRS):
        position[pair] = place_index
    lower = {}
    for column in range(5):
        diagonal = normal[position[column, column]] + RIDGE_WEIGHT
        for inner in range(column):
            diagonal = diagonal - lower[column, inner] * lower[column, inner]
        pivot_root = jnp.sqrt(diagonal)
        lower[column, column] = pivot_root
        for target in range(column + 1, 5):
            element = normal[position[column, target]]
            for inner in range(column):
                element = element - lower[target, inner] * lower[column, inner]
            lower[target, column] = element / pivot_root
    forward = []
    for target in range(5):
        residue = moments[target]
        for inner in range(target):
            residue = residue - lower[target, inner] * forward[inner]
        forward.append(residue / lower[target, target])
    coeffs = [None] * 5
    for target in reversed(range(5)):
        residue = forward[target]
        for inner in range(target + 1, 5):
            residue = residue - lower[inner, target] * coeffs[inner]
        coeffs[target] = residue / lower[target, target]
    return coeffs[0] + coeffs[3] * math.cos(MONTH_ANGLE) + coeffs[4] * math.sin(MONTH_ANGLE)


def regroup(values_four, meta_four, bands, band_levels):
    tiles = values_four.shape[2]
    width = values_four.shape[3]
    values_flat = values_four.reshape(2, bands, band_levels, tiles, width).transpose(0, 2, 1, 3, 4)
    values_flat = values_flat.reshape(2, band_levels, bands * tiles, width)
    meta_flat = meta_four.reshape(6, 1, bands * tiles, width)
    return (
        lax.all_to_all(values_flat, ("band", "tile"), split_axis=2, concat_axis=3, tiled=True),
        lax.all_to_all(meta_flat, ("band", "tile"), split_axis=2, concat_axis=3, tiled=True),
    )


def body(obs_values, obs_place, obs_depth, node_place, neighbours, counts):
    bands = lax.axis_size("band")
    tiles = lax.axis_size("tile")
    levels_all = obs_values.shape[1]
    band_levels = levels_all // bands
    slots = obs_values.shape[2] // tiles
    meta = profile_rows(obs_place, obs_depth)
    values_four = obs_values.reshape(2, levels_all, tiles, slots)
    meta_four = jnp.broadcast_to(meta.reshape(6, 1, tiles, slots), (6, bands, tiles, slots))
    values_got, meta_got = regroup(values_four, meta_four, bands, band_levels)
    combined = jnp.concatenate(
        [values_got.reshape(2 * band_levels, -1), meta_got.reshape(6, -1)], axis=0
    )
    extended = padded(combined, (("tile", 1),), combined.shape[1])
    level_ids = (
        lax.axis_index("band") * band_levels + jnp.arange(band_levels, dtype=jnp.int32)
    ).astype(jnp.float32)
    node_count = neighbours.shape[0]
    fan_total = neighbours.shape[1]
    node_step = math.gcd(node_count, 128)
    fan_step = math.gcd(fan_total, 256)
    frames_all = node_frames(node_place[0], node_place[1])

    def one_block(start_row):
        lists_block = lax.dynamic_slice_in_dim(neighbours, start_row, node_step, 0)
        count_block = lax.dynamic_slice_in_dim(counts, start_row, node_step, 0)
        frame_block = [
            lax.dynamic_slice_in_dim(part_rows, start_row, node_step, 0)[:, None]
            for part_rows in frames_all
        ]

        def add_fan(fan_block, totals):
            fan_start = fan_block * fan_step
            fan_ids = lax.dynamic_slice_in_dim(lists_block, fan_start, fan_step, 1)
            picked = jnp.take(extended, fan_ids, axis=1)
            positions = fan_start + jnp.arange(fan_step, dtype=jnp.int32)
            valid_mask = (positions[None, :] < count_block[:, None]).astype(jnp.float32)
            normal, moments = block_terms(picked, frame_block, valid_mask, level_ids)
            return (totals[0] + normal, totals[1] + moments)

        start_totals = (
            jnp.zeros((15, band_levels, node_step), jnp.float32),
            jnp.zeros((5, 2, band_levels, node_step), jnp.float32),
        )
        trip_count = fan_total // fan_step
        normal, moments = lax.fori_loop(0, trip_count, add_fan, start_totals)
        return solve_fit(normal, moments)

    starts = jnp.arange(node_count // node_step, dtype=jnp.int32) * node_step
    mapped = lax.map(one_block, starts)
    return mapped.transpose(1, 2, 0, 3).reshape(2, band_levels, node_count)


def solution(mesh):
    return jax.shard_map(
        body,
        mesh=mesh,
        in_specs=(
            P(None, None, ("band", "tile")),
            P(None, ("band", "tile")),
            P(("band", "tile")),
            P(None, "tile"),
            P("tile", None),
            P("tile"),
        ),
        out_specs=P(None, "band", "tile"),
        check_vma=False,
    )
```

profile of v0, /device:TPU:0, one launch (start us, length us, event | category | flops | bytes accessed | tf_op | source)
XLA Modules:
  0.0 707.9 jit_solution(144820464089105379)
XLA Ops:
  0.0 1.7 sine_reduce_fusion
  3.8 1.6 reduce.21
  5.5 0.9 reshape.1042
  6.4 11.2 %all-to-all-start.1 = ((f32[128,1,384]{2,1,0:T(1,128)}), f32[128,1,384]{2,1,0:T(1,128)S(1)}, u32[]{:S(2)}, u32[]{:S(2)}) async-start(f32[128,1,384]{2,1,0:T(1,128)} %reshape.1042), calls=%async_computation.1 | async-start | bytes 393216 | tf_op jit(solution)/shard_map/all_to_all | solution.py:134
  18.6 1.4 reshape.1040
  20.1 7.5 %all-to-all-done.1 = f32[128,1,384]{2,1,0:T(1,128)S(1)} async-done(((f32[128,1,384]{2,1,0:T(1,128)}), f32[128,1,384]{2,1,0:T(1,128)S(1)}, u32[]{:S(2)}, u32[]{:S(2)}) %all-to-all-start.1) | async-done | bytes 196640 | tf_op jit(solution)/shard_map/all_to_all | solution.py:134
  27.6 4.8 all-to-all-start
  32.4 1.1 reduce.22
  34.2 11.8 %all-to-all-done = f32[128,1,1024]{2,1,0:T(1,128)S(1)} async-done(((f32[128,1,1024]{2,1,0:T(1,128)}), f32[128,1,1024]{2,1,0:T(1,128)S(1)}, u32[]{:S(2)}, u32[]{:S(2)}) %all-to-all-start) | async-done | bytes 524320 | tf_op jit(solution)/shard_map/all_to_all | solution.py:133
  45.9 1.9 reduce.20
  49.0 5.1 collective-permute-start.1
  55.3 8.5 %collective-permute-done = f32[22,8192]{1,0:T(8,128)S(1)} collective-permute-done((f32[22,8192]{1,0:T(8,128)S(1)}, f32[22,8192]{1,0:T(8,128)S(1)}, u32[]{:S(2)}, u32[]{:S(2)}) %collective-permute-start) | collective-permute-done | bytes 720928 | tf_op jit(solution)/shard_map/ppermute | solution.py:25
  63.7 0.9 copy-done.2
  64.6 1.5 pad_maximum_fusion
  66.1 7.0 copy.166
  73.2 631.0 %while.24 = (s32[]{:T(128)}, f32[15,8,128]{0,1,2:T(8,128)}, f32[5,2,8,128]{0,2,1,3:T(8,128)}, s32[128,1024]{1,0:T(8,128)}, f32[22,24576]{0,1:T(8,128)}, /*index=...) while((s32[]{:T(128)}, f32[15,8,128]{0,1,2:T(8,128)}, ...), condition=%wide.region_1.2_spmd.clone, body=%wide.region_0.1_spmd.clone.sunk | while | flops 82397456 | bytes 39468940 | solution.py:183
  73.2 0.9 fusion.74
  74.2 113.6 %gather_fusion = f32[32768,22]{1,0:T(8,128)} fusion(f32[22,24576]{0,1:T(8,128)} %get-tuple-element.696, s32[32768]{0:T(1024)S(1)} %broadcast_clamp_fusion.2), kind=kCustom, calls=%fused_computation.clone.clone.1 | custom fusion | bytes 5898240 | tf_op jit(solution)/shard_map/while/body/eval_jaxpr/while/body/eval_jaxpr/jit(_take)/gather | solution.py:172
  187.8 11.4 %copy.217 = f32[128,256,22]{1,0,2:T(8,128)} copy(f32[128,256,22]{2,1,0:T(8,128)} %bitcast.176) | data formatting | bytes 5767168 | tf_op jit(solution)/shard_map/while/body/eval_jaxpr/while/body/eval_jaxpr/jit(_take)/gather | solution.py:172
  199.2 0.9 compare_and_fusion.2
  200.2 2.2 select_bitcast_fusion.2
  202.3 1.5 constant_dynamic-update-slice_fusion.26
  203.8 0.8 constant_dynamic-update-slice_fusion.27
  204.6 1.5 constant_dynamic-update-slice_fusion.28
  210.2 1.2 compare_convert_fusion.2
  211.3 1.6 slice.454
  212.9 6.5 fusion.76
  226.1 4.5 fusion.75
  230.6 0.9 fusion.74
  231.7 113.6 %gather_fusion = f32[32768,22]{1,0:T(8,128)} fusion(f32[22,24576]{0,1:T(8,128)} %get-tuple-element.696, s32[32768]{0:T(1024)S(1)} %broadcast_clamp_fusion.2), kind=kCustom, calls=%fused_computation.clone.clone.1 | custom fusion | bytes 5898240 | tf_op jit(solution)/shard_map/while/body/eval_jaxpr/while/body/eval_jaxpr/jit(_take)/gather | solution.py:172
  345.2 11.4 %copy.217 = f32[128,256,22]{1,0,2:T(8,128)} copy(f32[128,256,22]{2,1,0:T(8,128)} %bitcast.176) | data formatting | bytes 5767168 | tf_op jit(solution)/shard_map/while/body/eval_jaxpr/while/body/eval_jaxpr/jit(_take)/gather | solution.py:172
  356.7 0.9 compare_and_fusion.2
  357.6 2.2 select_bitcast_fusion.2
  359.8 1.5 constant_dynamic-update-slice_fusion.26
  361.3 0.8 constant_dynamic-update-slice_fusion.27
  362.0 1.5 constant_dynamic-update-slice_fusion.28
  367.6 1.2 compare_convert_fusion.2
  368.8 1.6 slice.454
  370.4 6.8 fusion.76
  383.9 4.6 fusion.75
  388.5 0.9 fusion.74
  389.5 113.6 %gather_fusion = f32[32768,22]{1,0:T(8,128)} fusion(f32[22,24576]{0,1:T(8,128)} %get-tuple-element.696, s32[32768]{0:T(1024)S(1)} %broadcast_clamp_fusion.2), kind=kCustom, calls=%fused_computation.clone.clone.1 | custom fusion | bytes 5898240 | tf_op jit(solution)/shard_map/while/body/eval_jaxpr/while/body/eval_jaxpr/jit(_take)/gather | solution.py:172
  503.1 11.4 %copy.217 = f32[128,256,22]{1,0,2:T(8,128)} copy(f32[128,256,22]{2,1,0:T(8,128)} %bitcast.176) | data formatting | bytes 5767168 | tf_op jit(solution)/shard_map/while/body/eval_jaxpr/while/body/eval_jaxpr/jit(_take)/gather | solution.py:172
  514.5 0.9 compare_and_fusion.2
  515.5 2.2 select_bitcast_fusion.2
  517.6 1.5 constant_dynamic-update-slice_fusion.26
  519.9 1.5 constant_dynamic-update-slice_fusion.28
  525.5 1.2 compare_convert_fusion.2
  526.7 1.6 slice.454
  528.2 6.8 fusion.76
  541.8 4.6 fusion.75
  546.4 0.9 fusion.74
  547.4 113.6 %gather_fusion = f32[32768,22]{1,0:T(8,128)} fusion(f32[22,24576]{0,1:T(8,128)} %get-tuple-element.696, s32[32768]{0:T(1024)S(1)} %broadcast_clamp_fusion.2), kind=kCustom, calls=%fused_computation.clone.clone.1 | custom fusion | bytes 5898240 | tf_op jit(solution)/shard_map/while/body/eval_jaxpr/while/body/eval_jaxpr/jit(_take)/gather | solution.py:172
  661.0 11.4 %copy.217 = f32[128,256,22]{1,0,2:T(8,128)} copy(f32[128,256,22]{2,1,0:T(8,128)} %bitcast.176) | data formatting | bytes 5767168 | tf_op jit(solution)/shard_map/while/body/eval_jaxpr/while/body/eval_jaxpr/jit(_take)/gather | solution.py:172
  672.4 0.9 compare_and_fusion.2
  673.3 2.2 select_bitcast_fusion.2
  675.5 1.5 constant_dynamic-update-slice_fusion.26
  677.8 1.5 constant_dynamic-update-slice_fusion.28
  683.3 1.2 compare_convert_fusion.2
  684.5 1.6 slice.454
  686.1 6.8 fusion.76
  699.7 4.6 fusion.75
  704.2 1.2 copy.168
  705.5 1.7 copy.167
  (136 shorter events, 52.3 us)
Async XLA Ops:
  0.0 17.6 %copy-start.3 = (f32[2,32,2048]{2,1,0:T(8,128)S(1)}, f32[2,32,2048]{2,1,0:T(8,128)}, u32[]{:S(2)}) copy-start(f32[2,32,2048]{2,1,0:T(8,128)} %param.8) | copy-start | bytes 1572868
  6.4 21.2 %all-to-all-start.1 = ((f32[128,1,384]{2,1,0:T(1,128)}), f32[128,1,384]{2,1,0:T(1,128)S(1)}, u32[]{:S(2)}, u32[]{:S(2)}) async-start(f32[128,1,384]{2,1,0:T(1,128)} %reshape.1042), calls=%async_computation.1 | async-start | bytes 393216 | tf_op jit(solution)/shard_map/all_to_all | solution.py:134
  27.6 18.3 %all-to-all-start = ((f32[128,1,1024]{2,1,0:T(1,128)}), f32[128,1,1024]{2,1,0:T(1,128)S(1)}, u32[]{:S(2)}, u32[]{:S(2)}) async-start(f32[128,1,1024]{2,1,0:T(1,128)} %reshape.1040), calls=%async_computation | async-start | bytes 1048576 | tf_op jit(solution)/shard_map/all_to_all | solution.py:133
  48.5 5.6 copy-start.4
  48.9 14.8 %collective-permute-start = (f32[22,8192]{1,0:T(8,128)S(1)}, f32[22,8192]{1,0:T(8,128)S(1)}, u32[]{:S(2)}, u32[]{:S(2)}) collective-permute-start(f32[22,8192]{1,0:T(8,128)S(1)} %constant_dynamic-update-slice_fusion.16), channel_id=1, source_target_pairs={{0,1},{1,2},{2,3},{3,4},{4,5},{5,6},{6,7},{7,8},{8,9},{9,10},{10,1... | collective-permute-start | bytes 2162696 | tf_op jit(solution)/shard_map/ppermute | solution.py:25
  49.0 15.6 %collective-permute-start.1 = (f32[22,8192]{1,0:T(8,128)S(1)}, f32[22,8192]{1,0:T(8,128)}, u32[]{:S(2)}, u32[]{:S(2)}) collective-permute-start(f32[22,8192]{1,0:T(8,128)S(1)} %constant_dynamic-update-slice_fusion.16), channel_id=1, source_target_pairs={{1,0},{2,1},{3,2},{4,3},{5,4},{6,5},{7,6},{8,7},{9,8},{10,9},{11,1... | collective-permute-start | bytes 2162696 | tf_op jit(solution)/shard_map/ppermute | solution.py:28
  63.7 0.9 copy-start.2
  209.5 0.7 copy-start
  219.4 6.8 copy-start.1
  367.0 0.7 copy-start
  377.1 6.8 copy-start.1
  524.8 0.7 copy-start
  535.0 6.8 copy-start.1
  682.7 0.7 copy-start
  692.9 6.8 copy-start.1
where the time goes:
time: 709 us; the launch traced here: 708 us
  local copies, waits for them, and re-layouts  535 us (75%)
  other arithmetic  78.6 us (11%)
  matrix products  45 us (6%)
  waiting for transfers between devices  27.8 us (4%)
  starting transfers between devices  21.1 us (3%)
    gather x8, local copies, waits for them, and re-layouts, add_fan(): picked = jnp.take(extended, fan_ids, axis=1)  500 us
    while x56, other arithmetic  45.9 us
    dot_general x4, matrix products, block_terms(): moments = jnp.einsum('pnk,vlnk->pvln', weighted, values, precision=HIGHEST)  26.8 us
    dot_general x4, matrix products, block_terms(): normal = jnp.einsum('pnk,lnk->pln', crossed, inside, precision=HIGHEST)  18.2 us
  transfers between devices with their start and end apart: 4, of which 3 were waited for; matrix products, arithmetic and copies ran while one was open for 1% of the time, Pallas kernels for 0%

commit v1 on v0

v1 whole, which is shorter than its diff:
```python
import math

import jax
import jax.numpy as jnp
from jax import lax
from jax.experimental import pallas as pl
from jax.experimental.pallas import tpu as pltpu
from jax.sharding import PartitionSpec as P

MONTH_ANGLE = -11.0 * math.pi / 12.0
BF = jnp.bfloat16
F32 = jnp.float32
E4 = jnp.float8_e4m3fn
NT_DIMS = (((1,), (1,)), ((), ()))
LANES = 128
GROUPS = 19
VMEM_LIMIT = 60 * 2**20


def list_rows(nb_ref, cnt_ref, hi_ref, lo_ref):
    nb = nb_ref[...]
    valid = lax.broadcasted_iota(jnp.int32, nb.shape, 1) < cnt_ref[...]
    hi_ref[...] = jnp.where(valid, lax.shift_right_logical(nb, 7), -1).astype(F32)
    lo_ref[...] = lax.bitwise_and(nb, LANES - 1).astype(F32)


def count_node(n, hi_ref, lo_ref, m_ref):
    fan = hi_ref.shape[1]
    tiles = m_ref.shape[1]
    hi_ids = lax.broadcasted_iota(jnp.int32, (tiles, fan), 0).astype(BF)
    lo_ids = lax.broadcasted_iota(jnp.int32, (LANES, fan), 0).astype(BF)
    hi = jnp.broadcast_to(hi_ref[pl.ds(n, 1), :], (16, fan)).astype(BF)
    lo = jnp.broadcast_to(lo_ref[pl.ds(n, 1), :], (16, fan)).astype(BF)
    hi = jnp.concatenate([hi] * (tiles // 16), 0)
    lo = jnp.concatenate([lo] * (LANES // 16), 0)
    one, zero = jnp.ones((), BF), jnp.zeros((), BF)
    hot_hi = jnp.where(hi_ids == hi, one, zero).astype(E4)
    hot_lo = jnp.where(lo_ids == lo, one, zero).astype(E4)
    m_ref[pl.ds(n, 1)] = lax.dot_general(hot_hi, hot_lo, NT_DIMS, preferred_element_type=F32)[None]


def split2(x):
    high = x.astype(BF)
    return high, (x - high.astype(F32)).astype(BF)


def split3(x):
    high = x.astype(BF)
    rest = x - high.astype(F32)
    mid = rest.astype(BF)
    return high, mid, (rest - mid.astype(F32)).astype(BF)


def node_left(node_x, node_y, node_z):
    scale = 8.0 * math.log2(math.e)
    col = lax.broadcasted_iota(jnp.int32, (node_x.shape[0], LANES), 1)
    row = lax.bitwise_and(col, 7)
    vals = jnp.where(
        row == 0,
        node_x * scale,
        jnp.where(row == 1, node_y * scale, jnp.where(row == 2, node_z * scale, jnp.where(row == 6, -scale, 0.0))),
    )
    high, mid, low = split3(vals)
    block = lax.shift_right_logical(col, 3)
    high, mid, low = high.astype(F32), mid.astype(F32), low.astype(F32)
    part = jnp.where(
        (block == 0) | (block == 3) | (block == 5),
        high,
        jnp.where((block == 1) | (block == 4), mid, jnp.where(block == 2, low, 0.0)),
    )
    return part.astype(BF)


def meta_features(meta):
    dense = jnp.swapaxes(meta, 0, 1)
    x, y, z, c, s = (dense[i] for i in range(5))
    return [x, y, z, c, s, x * x, x * y, x * z, y * y, y * z, x * c, y * c, z * c, x * s, y * s, z * s, c * c, c * s]


def ext_block(blk, level_base, ext_ref, m_ref, left, gh_ref, gl_ref, fh_ref, fl_ref, acc_ref):
    nodes = m_ref.shape[0]
    start = pl.multiple_of(blk * 8, 8)
    meta = ext_ref[pl.ds(start, 8), 16:24, :]
    prods = meta_features(meta)
    for index, prod in enumerate(prods):
        high = prod.astype(BF).astype(F32)
        gh_ref[index] = high
        gl_ref[index] = prod - high
    level = (lax.broadcasted_iota(jnp.int32, (8, LANES), 0) + level_base).astype(F32)
    zero = jnp.zeros((8, LANES), F32)
    profile_parts = []
    for t in range(8):
        cols = pl.ds(t * LANES, LANES)
        rows = ext_ref[start + t]
        tile_meta = rows[16:24]
        inside = level < jnp.broadcast_to(tile_meta[5:6], (8, LANES))
        high, mid, low = split3(tile_meta)
        high, mid, low = high.astype(F32), mid.astype(F32), low.astype(F32)
        profile_parts.append(jnp.concatenate([high, high, high, mid, mid, low], 0).astype(BF))
        highs = [jnp.where(inside, 1.0, 0.0)]
        lows = [zero]
        for index in range(GROUPS - 1):
            highs.append(jnp.where(inside, jnp.broadcast_to(gh_ref[index, t : t + 1, :], (8, LANES)), zero))
            lows.append(jnp.where(inside, jnp.broadcast_to(gl_ref[index, t : t + 1, :], (8, LANES)), zero))
        factors = [jnp.broadcast_to(tile_meta[i : i + 1], (8, LANES)) for i in range(5)]
        for v in range(2):
            value = jnp.where(inside, rows[8 * v : 8 * v + 8], zero)
            for term in [value] + [value * factor for factor in factors]:
                high = term.astype(BF).astype(F32)
                highs.append(high)
                lows.append(term - high)
        highs.append(zero)
        lows.append(zero)
        for pair in range(16):
            part = pl.ds(pair * 16, 16)
            fh_ref[part, cols] = jnp.concatenate(highs[2 * pair : 2 * pair + 2], 0).astype(BF)
            fl_ref[part, cols] = jnp.concatenate(lows[2 * pair : 2 * pair + 2], 0).astype(BF)
    right = jnp.concatenate(profile_parts, 1)
    power = lax.dot_general(left[:, :48], right, (((1,), (0,)), ((), ())), preferred_element_type=F32)
    counted = m_ref[:, pl.ds(start, 8), :]
    counted = jnp.swapaxes(counted.reshape(nodes // 8, 8, 8, LANES), 1, 2)
    counted = jnp.concatenate([counted[:, t].reshape(nodes, LANES) for t in range(8)], 1)
    weight = jnp.exp2(power) * counted
    w_high, w_low = split2(weight)
    both = jnp.concatenate([w_high, w_low], 0)
    first = lax.dot_general(fh_ref[...], both, NT_DIMS, preferred_element_type=F32)
    second = lax.dot_general(fl_ref[...], w_high, NT_DIMS, preferred_element_type=F32)
    acc_ref[...] += first[:, :nodes] + first[:, nodes:] + second


def fit_nodes(acc_ref, frame, out_ref):
    nodes = acc_ref.shape[1]
    ex, ey, qx, qy, qz = (jnp.broadcast_to(2.0 * part, (8, nodes)) for part in frame)
    sums = [acc_ref[8 * i : 8 * i + 8, :] for i in range(GROUPS + 12)]
    s1, sx, sy, sz, sc, ss, sxx, sxy, sxz, syy, syz, sxc, syc, szc, sxs, sys_, szs, scc, scs = sums[:GROUPS]
    szz = s1 - sxx - syy
    normal = {
        (0, 0): s1,
        (0, 1): ex * sx + ey * sy,
        (0, 2): qx * sx + qy * sy + qz * sz,
        (0, 3): sc,
        (0, 4): ss,
        (1, 1): ex * ex * sxx + 2.0 * ex * ey * sxy + ey * ey * syy,
        (1, 2): ex * qx * sxx + (ex * qy + ey * qx) * sxy + ey * qy * syy + ex * qz * sxz + ey * qz * syz,
        (1, 3): ex * sxc + ey * syc,
        (1, 4): ex * sxs + ey * sys_,
        (2, 2): qx * qx * sxx + qy * qy * syy + qz * qz * szz + 2.0 * (qx * qy * sxy + qx * qz * sxz + qy * qz * syz),
        (2, 3): qx * sxc + qy * syc + qz * szc,
        (2, 4): qx * sxs + qy * sys_ + qz * szs,
        (3, 3): scc,
        (3, 4): scs,
        (4, 4): s1 - scc,
    }
    lower = {}
    inverse = []
    for column in range(5):
        diagonal = normal[column, column] + 1.0
        for inner in range(column):
            diagonal = diagonal - lower[column, inner] * lower[column, inner]
        inverse.append(1.0 / jnp.sqrt(diagonal))
        for target in range(column + 1, 5):
            element = normal[column, target]
            for inner in range(column):
                element = element - lower[target, inner] * lower[column, inner]
            lower[target, column] = element * inverse[column]
    for v in range(2):
        m1, mx, my, mz, mc, ms = sums[GROUPS + 6 * v : GROUPS + 6 * v + 6]
        moments = [m1, ex * mx + ey * my, qx * mx + qy * my + qz * mz, mc, ms]
        forward = []
        for target in range(5):
            residue = moments[target]
            for inner in range(target):
                residue = residue - lower[target, inner] * forward[inner]
            forward.append(residue * inverse[target])
        coeffs = [None] * 5
        for target in reversed(range(5)):
            residue = forward[target]
            for inner in range(target + 1, 5):
                residue = residue - lower[inner, target] * coeffs[inner]
            coeffs[target] = residue * inverse[target]
        out_ref[v] = coeffs[0] + coeffs[3] * math.cos(MONTH_ANGLE) + coeffs[4] * math.sin(MONTH_ANGLE)


def node_frame(longitude, latitude):
    sin_lat, cos_lat = jnp.sin(latitude), jnp.cos(latitude)
    sin_lon, cos_lon = jnp.sin(longitude), jnp.cos(longitude)
    point = (cos_lat * cos_lon, cos_lat * sin_lon, sin_lat)
    frame = (-sin_lon, cos_lon, -sin_lat * cos_lon, -sin_lat * sin_lon, cos_lat)
    return point, frame


def fit_kernel(nb_ref, cnt_ref, place_ref, place_t_ref, ext_ref, out_ref, hi_ref, lo_ref, m_ref, gh_ref, gl_ref, fh_ref, fl_ref, acc_ref):
    nodes = nb_ref.shape[0]
    list_rows(nb_ref, cnt_ref, hi_ref, lo_ref)

    def count_step(n, carry):
        count_node(n, hi_ref, lo_ref, m_ref)
        return carry

    lax.fori_loop(0, nodes, count_step, 0, unroll=8)
    acc_ref[...] = jnp.zeros_like(acc_ref)
    point, _ = node_frame(place_t_ref[:, 0:1], place_t_ref[:, 1:2])
    left = node_left(*point)
    level_base = lax.axis_index("band") * 8

    def block_step(blk, carry):
        ext_block(blk, level_base, ext_ref, m_ref, left, gh_ref, gl_ref, fh_ref, fl_ref, acc_ref)
        return carry

    lax.fori_loop(0, m_ref.shape[1] // 8, block_step, 0)
    _, frame = node_frame(place_ref[0:1, :], place_ref[1:2, :])
    fit_nodes(acc_ref, frame, out_ref)


def fit_call(neighbours, counts, node_place, ext):
    nodes, fan = neighbours.shape
    tiles = ext.shape[0]
    vmem = pl.BlockSpec(memory_space=pltpu.VMEM)
    return pl.pallas_call(
        fit_kernel,
        out_shape=jax.ShapeDtypeStruct((2, 8, nodes), F32),
        in_specs=[vmem] * 5,
        out_specs=vmem,
        scratch_shapes=[
            pltpu.VMEM((nodes, fan), F32),
            pltpu.VMEM((nodes, fan), F32),
            pltpu.VMEM((nodes, tiles, LANES), F32),
            pltpu.VMEM((GROUPS - 1, 8, LANES), F32),
            pltpu.VMEM((GROUPS - 1, 8, LANES), F32),
            pltpu.VMEM((256, 8 * LANES), BF),
            pltpu.VMEM((256, 8 * LANES), BF),
            pltpu.VMEM((256, nodes), F32),
        ],
        compiler_params=pltpu.CompilerParams(vmem_limit_bytes=VMEM_LIMIT),
    )(neighbours, counts.reshape(nodes, 1), node_place, node_place.T, ext)


def profile_rows(obs_place, obs_depth):
    longitude, latitude, day_angle = obs_place[0], obs_place[1], obs_place[2]
    cos_lat = jnp.cos(latitude)
    return jnp.stack(
        [
            cos_lat * jnp.cos(longitude),
            cos_lat * jnp.sin(longitude),
            jnp.sin(latitude),
            jnp.cos(day_angle),
            jnp.sin(day_angle),
            obs_depth.astype(F32),
            jnp.ones_like(longitude),
            jnp.zeros_like(longitude),
        ]
    )


def body(obs_values, obs_place, obs_depth, node_place, neighbours, counts):
    bands = lax.axis_size("band")
    tiles = lax.axis_size("tile")
    levels = obs_values.shape[1] // bands
    slots = obs_values.shape[2] // tiles
    values = obs_values.reshape(2, bands, levels, tiles, slots).transpose(1, 3, 0, 2, 4).reshape(bands, tiles, 2 * levels, slots)
    meta = profile_rows(obs_place, obs_depth).reshape(8, tiles, slots).transpose(1, 0, 2)
    meta = jnp.broadcast_to(meta[None], (bands,) + meta.shape)
    rows = jnp.concatenate([values, meta], 2).reshape(bands * tiles, 2 * levels + 8, slots)
    got = lax.all_to_all(rows, ("band", "tile"), 0, 0, tiled=True)
    devices = got.shape[0]
    got = got.reshape(devices // 2, 2, 2 * levels + 8, slots).transpose(0, 2, 1, 3).reshape(devices // 2, 2 * levels + 8, 2 * slots)
    forward = [(i, (i + 1) % tiles) for i in range(tiles)]
    backward = [(t, s) for s, t in forward]
    low = lax.ppermute(got, "tile", forward)
    high = lax.ppermute(got, "tile", backward)
    ext = jnp.concatenate([low, got, high], 0)
    return fit_call(neighbours, counts, node_place, ext)


def solution(mesh):
    return jax.shard_map(
        body,
        mesh=mesh,
        in_specs=(
            P(None, None, ("band", "tile")),
            P(None, ("band", "tile")),
            P(("band", "tile")),
            P(None, "tile"),
            P("tile", None),
            P("tile"),
        ),
        out_specs=P(None, "band", "tile"),
        check_vma=False,
    )
```

time: 709 us -> 86.8 us (0.12)
  local copies, waits for them, and re-layouts: 535 us -> 7.59 us
  other arithmetic: 78.6 us -> 6.56 us
  matrix products: 45 us -> 0 us
  Pallas kernels: 0 us -> 31.6 us
  blocking collectives: 0 us -> 27.3 us
  waiting for transfers between devices: 27.8 us -> 8.21 us
  starting transfers between devices: 21.1 us -> 5.13 us
    gather x8 -> x0, local copies, waits for them, and re-layouts: 500 us -> none  [add_fan(): picked = jnp.take(extended, fan_ids, axis=1)]
    while x56 -> x0, other arithmetic: 45.9 us -> none
    dot_general x8 -> x0, matrix products: 45 us -> none  [the longest x4 26.8 us: block_terms(): moments = jnp.einsum('pnk,vlnk->pvln', weighted, values, precision=HIGHEST)]
    pallas_call x0 -> x1, Pallas kernels: none -> 31.6 us  [fit_call(): pl.pallas_call(fit_kernel, out_shape=jax.ShapeDtypeStruct((2, 8, nodes),...]
    all_to_all x0 -> x1, blocking collectives: none -> 27.3 us  [body(): got = lax.all_to_all(rows, ('band', 'tile'), 0, 0, tiled=True)]
    all_to_all x2 -> x0, waiting for transfers between devices: 19.3 us -> none  [the longest x1 11.8 us: regroup(): lax.all_to_all(values_flat, ('band', 'tile'), split_axis=2, concat_axis=3...]
    all_to_all x2 -> x0, starting transfers between devices: 16 us -> none  [the longest x1 11.2 us: regroup(): lax.all_to_all(meta_flat, ('band', 'tile'), split_axis=2, concat_axis=3,...]
    while x34 -> x0, local copies, waits for them, and re-layouts: 13.7 us -> none
  transfers between devices with their start and end apart: 4 -> 2, of which waited for: 3 -> 1; matrix products, arithmetic and copies ran while one was open for 1% -> 2% of each run, Pallas kernels for 0% -> 0%
where the time goes in v1:
time: 86.8 us; the launch traced here: 86.5 us
  Pallas kernels  31.6 us (36%)
  blocking collectives  27.3 us (31%)
  waiting for transfers between devices  8.21 us (9%)
  local copies, waits for them, and re-layouts  7.59 us (9%)
  other arithmetic  6.56 us (8%)
  starting transfers between devices  5.13 us (6%)
    pallas_call x1, Pallas kernels, fit_call(): pl.pallas_call(fit_kernel, out_shape=jax.ShapeDtypeStruct((2, 8, nodes),...  31.6 us
    all_to_all x1, blocking collectives, body(): got = lax.all_to_all(rows, ('band', 'tile'), 0, 0, tiled=True)  27.3 us
    ppermute x1, waiting for transfers between devices, body(): low = lax.ppermute(got, 'tile', forward)  8.2 us
    ppermute x1, starting transfers between devices, body(): high = lax.ppermute(got, 'tile', backward)  5.05 us
    all_to_all x1, other arithmetic, body(): got = lax.all_to_all(rows, ('band', 'tile'), 0, 0, tiled=True)  2.51 us
    unnamed x14, local copies, waits for them, and re-layouts  2.08 us
    reshape x2, local copies, waits for them, and re-layouts, body(): obs_values.reshape(2, bands, levels, tiles, slots).transpose(1, 3, 0, 2, 4)  2.07 us
  transfers between devices with their start and end apart: 2, of which 1 were waited for; matrix products, arithmetic and copies ran while one was open for 2% of the time, Pallas kernels for 0%

profile of v1, /device:TPU:0, one launch (start us, length us, event | category | flops | bytes accessed | tf_op | source)
XLA Modules:
  0.0 86.5 jit_solution(15085604767794095878)
XLA Ops:
  0.0 1.7 %sine_reduce_fusion = (f32[2048]{0:T(1024)S(1)}, f32[2048]{0:T(1024)S(1)}, f32[2048]{0:T(1024)S(1)}, f32[2048]{0:T(1024)S(1)}, f32[2048]{0:T(1024)S(1)}) fusion(f32[3,2048]{1,0:T(4,128)} %param.7), kind=kLoop, calls=%fused_computation.10 | loop fusion | flops 4096 | bytes 65536 | tf_op jit(solution)/shard_map/sin | solution.py:247
  1.7 0.1 stack.21
  1.8 0.1 stack.22
  1.8 0.1 stack.23
  1.9 0.1 stack.24
  2.0 0.1 stack.25
  2.0 0.7 convert_element_type.3
  2.7 0.1 stack.26
  2.9 0.1 copy.12
  3.0 1.5 %reshape.29 = f32[2,4,8,32,64]{4,3,2,1,0:T(8,128)S(1)} reshape(f32[2,32,2048]{2,1,0:T(8,128)} %param.6) | data formatting | bytes 1048576 | tf_op jit(solution)/shard_map/reshape | solution.py:260
  4.4 0.6 copy.11
  5.1 0.1 pad_maximum_fusion.1
  5.2 1.0 %reshape.59 = f32[128,1,1536]{2,1,0:T(1,128)S(1)} reshape(f32[128,24,64]{2,1,0:T(8,128)S(1)} %pad_maximum_fusion.1) | data formatting | bytes 1572864
  6.2 27.3 %all_to_all.5 = f32[128,1,1536]{2,1,0:T(1,128)S(1)} all-to-all(f32[128,1,1536]{2,1,0:T(1,128)S(1)} %reshape.59), channel_id=1, replica_groups=mesh['band'=4,'tile'=32] {'band','tile'}, dimensions={0} | all-to-all | bytes 1572864 | tf_op jit(solution)/shard_map/all_to_all | solution.py:264
  33.5 0.5 broadcast.18
  34.0 2.5 %reduce.20 = f32[128,1536]{1,0:T(8,128)S(1)} reduce(f32[128,1,1536]{2,1,0:T(1,128)S(1)} %all_to_all.5, f32[]{:T(128)} %broadcast.18), dimensions={1}, to_apply=%all_to_all.3.reduce_sub_computation | reduce | bytes 1572868 | tf_op jit(solution)/shard_map/all_to_all | solution.py:264
  36.5 0.3 reshape.60
  36.9 0.0 copy-start
  36.9 0.0 copy-start.1
  36.9 0.8 copy.13
  37.7 0.9 reshape.31
  38.6 0.1 collective-permute-start
  38.7 5.1 %collective-permute-start.1 = (f32[64,24,128]{2,1,0:T(8,128)S(1)}, f32[64,24,128]{2,1,0:T(8,128)S(1)}, u32[]{:S(2)}, u32[]{:S(2)}) collective-permute-start(f32[64,24,128]{2,1,0:T(8,128)S(1)} %reshape.31), channel_id=1, source_target_pairs={{1,0},{2,1},{3,2},{4,3},{5,4},{6,5},{7,6},{8,7},{9,8},{10,9},{11,1... | collective-permute-start | bytes 2359304 | tf_op jit(solution)/shard_map/ppermute | solution.py:270
  43.7 0.0 copy-done
  43.7 0.7 copy.10
  44.4 0.0 copy-done.1
  44.4 0.7 copy.14.cnt_ref
  45.2 8.2 %collective-permute-done = f32[64,24,128]{2,1,0:T(8,128)S(1)} collective-permute-done((f32[64,24,128]{2,1,0:T(8,128)S(1)}, f32[64,24,128]{2,1,0:T(8,128)S(1)}, u32[]{:S(2)}, u32[]{:S(2)}) %collective-permute-start) | collective-permute-done | bytes 786464 | tf_op jit(solution)/shard_map/ppermute | solution.py:269
  53.4 0.0 collective-permute-done.1
  53.4 1.6 %pad_maximum_fusion.ext_ref = f32[192,24,128]{2,1,0:T(8,128)} fusion(f32[64,24,128]{2,1,0:T(8,128)S(1)} %collective-permute-done.1, f32[64,24,128]{2,1,0:T(8,128)S(1)} %reshape.31, f32[64,24,128]{2,1,0:T(8,128)S(1)} %collective-permute-done), kind=kLoop, calls=%fused_computation | loop fusion | flops 1179648 | bytes 4718592 | tf_op jit(solution)/shard_map/concatenate | solution.py:271
  54.9 31.6 %shard_map.64 = f32[2,8,128]{2,1,0:T(8,128)} custom-call(s32[128,1024]{1,0:T(8,128)} %nb_ref.1, s32[128,1]{1,0:T(8,128)} %copy.14.cnt_ref, f32[2,128]{1,0:T(2,128)} %place_ref.1, f32[128,2]{1,0:T(8,128)} %bitcast.13, f32[192,24,128]{2,1,0:T(8,128)} %pad_maximum_fusion.ext_ref), custom_call_target="tpu_custom_call" | custom-call | tf_op jit(solution)/shard_map/pallas_call | solution.py:219
  (9 shorter events, 0.1 us)
Async XLA Ops:
  36.9 6.8 %copy-start = (f32[2,128]{1,0:T(2,128)S(1)}, f32[2,128]{1,0:T(2,128)}, u32[]{:S(2)}) copy-start(f32[2,128]{1,0:T(2,128)} %place_ref.1) | copy-start | bytes 3076
  36.9 7.6 %copy-start.1 = (s32[128]{0:T(128)S(1)}, s32[128]{0:T(128)}, u32[]{:S(2)}) copy-start(s32[128]{0:T(128)} %param.11) | copy-start | bytes 1540
  38.6 14.8 %collective-permute-start = (f32[64,24,128]{2,1,0:T(8,128)S(1)}, f32[64,24,128]{2,1,0:T(8,128)S(1)}, u32[]{:S(2)}, u32[]{:S(2)}) collective-permute-start(f32[64,24,128]{2,1,0:T(8,128)S(1)} %reshape.31), channel_id=1, source_target_pairs={{0,1},{1,2},{2,3},{3,4},{4,5},{5,6},{6,7},{7,8},{8,9},{9,10},{10,1... | collective-permute-start | bytes 2359304 | tf_op jit(solution)/shard_map/ppermute | solution.py:269
  38.7 14.7 %collective-permute-start.1 = (f32[64,24,128]{2,1,0:T(8,128)S(1)}, f32[64,24,128]{2,1,0:T(8,128)S(1)}, u32[]{:S(2)}, u32[]{:S(2)}) collective-permute-start(f32[64,24,128]{2,1,0:T(8,128)S(1)} %reshape.31), channel_id=1, source_target_pairs={{1,0},{2,1},{3,2},{4,3},{5,4},{6,5},{7,6},{8,7},{9,8},{10,9},{11,1... | collective-permute-start | bytes 2359304 | tf_op jit(solution)/shard_map/ppermute | solution.py:270

commit v2 on v1

--- a/solution.py
+++ b/solution.py
@@ -13,15 +13,28 @@
 E4 = jnp.float8_e4m3fn
 NT_DIMS = (((1,), (1,)), ((), ()))
 LANES = 128
+MESH = pl.DeviceIdType.MESH
 GROUPS = 19
 VMEM_LIMIT = 60 * 2**20
 
 
-def list_rows(nb_ref, cnt_ref, hi_ref, lo_ref):
+def list_rows(core, nb_ref, cnt_col, hi_ref, lo_ref):
     nb = nb_ref[...]
-    valid = lax.broadcasted_iota(jnp.int32, nb.shape, 1) < cnt_ref[...]
-    hi_ref[...] = jnp.where(valid, lax.shift_right_logical(nb, 7), -1).astype(F32)
-    lo_ref[...] = lax.bitwise_and(nb, LANES - 1).astype(F32)
+    valid = lax.broadcasted_iota(jnp.int32, nb.shape, 1).astype(F32) < cnt_col
+    segment = lax.shift_right_logical(nb, 13)
+    chip = lax.bitwise_and(lax.shift_right_logical(nb, 7), 63)
+    source_core = lax.bitwise_and(lax.shift_right_logical(nb, 6), 1)
+    slot = chip_slot(lax.shift_right_logical(chip, 4), lax.bitwise_and(lax.shift_right_logical(chip, 2), 3), lax.bitwise_and(chip, 3))
+    is_halo = segment == 2 * core
+    half = segment - 1 + core
+    hi = slot + jnp.where(is_halo, 128, jnp.where(source_core == core, 0, 64))
+    lo = jnp.where(is_halo, lax.bitwise_and(nb, 127), lax.bitwise_and(nb, 63) + 64 * half)
+    hi_ref[...] = jnp.where(valid, hi, -1).astype(F32)
+    lo_ref[...] = lo.astype(F32)
+
+
+def chip_slot(x, z, y):
+    return lax.bitwise_and(x + z + y, 3) * 16 + x * 4 + y
 
 
 def count_node(n, hi_ref, lo_ref, m_ref):
@@ -189,87 +202,199 @@
     return point, frame
 
 
-def fit_kernel(nb_ref, cnt_ref, place_ref, place_t_ref, ext_ref, out_ref, hi_ref, lo_ref, m_ref, gh_ref, gl_ref, fh_ref, fl_ref, acc_ref):
+def dense_rows(ref, row):
+    return jnp.concatenate([ref[row : row + 1, m * LANES : (m + 1) * LANES] for m in range(ref.shape[1] // LANES)], 0)
+
+
+def profile_meta(place_ref, depth_ref):
+    longitude, latitude, day_angle = (dense_rows(place_ref, row) for row in range(3))
+    cos_lat = jnp.cos(latitude)
+    rows = [
+        cos_lat * jnp.cos(longitude),
+        cos_lat * jnp.sin(longitude),
+        jnp.sin(latitude),
+        jnp.cos(day_angle),
+        jnp.sin(day_angle),
+        dense_rows(depth_ref, 0).astype(F32),
+        jnp.ones_like(cos_lat),
+        jnp.zeros_like(cos_lat),
+    ]
+    return jnp.swapaxes(jnp.stack(rows, 0), 0, 1)
+
+
+def full_kernel(
+    values_ref, place_ref, depth_ref, node_ref, nb_ref, cnt_ref, out_ref,
+    meta_ref, sib_values_ref, sib_meta_ref, own_ref, halo_ref, ext_ref,
+    hi_ref, lo_ref, m_ref, gh_ref, gl_ref, fh_ref, fl_ref, acc_ref,
+    send_own, send_halo, recv, pass_send, sib_send, sib_recv,
+):
+    x = lax.axis_index("band")
+    tile = lax.axis_index("tile")
+    core = lax.rem(tile, 2)
+    chip = lax.div(tile, 2)
+    z, y = lax.div(chip, 4), lax.rem(chip, 4)
+    sibling = {"tile": tile + 1 - 2 * core}
+    mine = chip_slot(x, z, y)
+    phase = lax.rem(x + z + y, 4)
     nodes = nb_ref.shape[0]
-    list_rows(nb_ref, cnt_ref, hi_ref, lo_ref)
-
-    def count_step(n, carry):
-        count_node(n, hi_ref, lo_ref, m_ref)
+
+    def partner(index):
+        dx, dy = lax.rem(lax.div(index, 4), 4), lax.rem(index, 4)
+        dz = lax.rem(lax.div(index, 16) + 8 - dx - dy, 4)
+        other_x, other_z, other_y = lax.rem(x + dx, 4), lax.rem(z + dz, 4), lax.rem(y + dy, 4)
+        pair = other_z * 4 + other_y
+        return other_x * 16 + pair, {"band": other_x, "tile": 2 * pair + core}
+
+    barrier = pltpu.get_barrier_semaphore()
+
+    def greet(index, carry):
+        _, device = partner(index)
+        pl.semaphore_signal(barrier, inc=1, device_id=device, device_id_type=MESH)
         return carry
 
-    lax.fori_loop(0, nodes, count_step, 0, unroll=8)
+    lax.fori_loop(1, 64, greet, 0)
+    pl.semaphore_signal(barrier, inc=1, device_id=sibling, device_id_type=MESH)
+
+    meta_ref[...] = profile_meta(place_ref, depth_ref)
+    for b in range(4):
+        for m in range(16):
+            for v in range(2):
+                own_ref[b * 16 + m, 8 * v : 8 * v + 8, :] = values_ref[v, 8 * b : 8 * b + 8, m * LANES : (m + 1) * LANES]
+            own_ref[b * 16 + m, 16:24, :] = meta_ref[m]
+    point, frame = node_frame(node_ref[0:1, :], node_ref[1:2, :])
+    packed = jnp.concatenate(list(point) + [cnt_ref[...].astype(F32)] + [jnp.zeros((124, nodes), F32)], 0)
+    columns = packed.T
+    left = node_left(columns[:, 0:1], columns[:, 1:2], columns[:, 2:3])
+    list_rows(core, nb_ref, columns[:, 3:4], hi_ref, lo_ref)
     acc_ref[...] = jnp.zeros_like(acc_ref)
-    point, _ = node_frame(place_t_ref[:, 0:1], place_t_ref[:, 1:2])
-    left = node_left(*point)
-    level_base = lax.axis_index("band") * 8
-
-    def block_step(blk, carry):
-        ext_block(blk, level_base, ext_ref, m_ref, left, gh_ref, gl_ref, fh_ref, fl_ref, acc_ref)
+
+    pl.semaphore_wait(barrier, 64)
+    sib_copies = [
+        pltpu.make_async_remote_copy(values_ref, sib_values_ref, sib_send.at[0], sib_recv.at[0], device_id=sibling, device_id_type=MESH),
+        pltpu.make_async_remote_copy(meta_ref, sib_meta_ref, sib_send.at[1], sib_recv.at[1], device_id=sibling, device_id_type=MESH),
+    ]
+    for copy in sib_copies:
+        copy.start()
+
+    def send(buffer, base, send_sem):
+        def step(index, carry):
+            unit, device = partner(index)
+            pltpu.make_async_remote_copy(
+                buffer.at[unit], ext_ref.at[16 * base + mine], send_sem, recv.at[base + phase], device_id=device, device_id_type=MESH
+            ).start()
+            return carry
+
+        lax.fori_loop(1, 64, step, 0)
+
+    def keep(buffer, base):
+        return pltpu.make_async_copy(buffer.at[x * 16 + chip], ext_ref.at[16 * base + mine], recv.at[base + phase])
+
+    def group(index):
+        return ext_ref.at[pl.ds(pl.multiple_of(index * 16, 16), 16)]
+
+    def wait_group(index):
+        pltpu.make_async_copy(group(index), group(index), recv.at[index]).wait()
+
+    keep(own_ref, 0).start()
+    send(own_ref, 0, send_own)
+
+    def send_halos():
+        for copy in sib_copies:
+            copy.wait_recv()
+        from_own = lax.shift_right_logical(lax.broadcasted_iota(jnp.int32, (8, LANES), 1), 6) == core
+
+        def step(m, carry):
+            other = lax.rem(m + 15 + 2 * core, 16)
+            cols = pl.ds(pl.multiple_of(other * LANES, LANES), LANES)
+            meta = jnp.where(from_own, pltpu.roll(meta_ref[other], 64, 1), sib_meta_ref[other])
+            for b in range(4):
+                unit = b * 16 + m
+                for v in range(2):
+                    mine_rows = values_ref[v, 8 * b : 8 * b + 8, cols]
+                    their_rows = sib_values_ref[v, 8 * b : 8 * b + 8, cols]
+                    halo_ref[unit, 8 * v : 8 * v + 8, :] = jnp.where(from_own, pltpu.roll(mine_rows, 64, 1), their_rows)
+                halo_ref[unit, 16:24, :] = meta
+            return carry
+
+        lax.fori_loop(0, 16, step, 0)
+        keep(halo_ref, 8).start()
+        send(halo_ref, 8, send_halo)
+
+    def pass_copy(k):
+        return pltpu.make_async_remote_copy(
+            group(k), group(4 + k), pass_send.at[k], recv.at[4 + k], device_id=sibling, device_id_type=MESH
+        )
+
+    def pass_group(order):
+        k = lax.rem(phase + 4 - order, 4)
+        wait_group(k)
+        pass_copy(k).start()
+
+    def count_step(step, carry):
+        for n in range(8):
+            count_node(step * 8 + n, hi_ref, lo_ref, m_ref)
+        pl.when(step == 1)(send_halos)
+        pl.when((step >= 9) & (lax.rem(step, 2) == 1))(lambda: pass_group(lax.div(step - 9, 2)))
         return carry
 
-    lax.fori_loop(0, m_ref.shape[1] // 8, block_step, 0)
-    _, frame = node_frame(place_ref[0:1, :], place_ref[1:2, :])
+    lax.fori_loop(0, nodes // 8, count_step, 0)
+    level_base = x * 8
+
+    def pair_step(pair, carry):
+        k = lax.rem(phase + 4 - lax.rem(pair, 4), 4)
+        index = lax.div(pair, 4) * 4 + k
+        pl.when(pair >= 4)(lambda: wait_group(index))
+
+        def block_step(part, inner):
+            ext_block(2 * index + part, level_base, ext_ref, m_ref, left, gh_ref, gl_ref, fh_ref, fl_ref, acc_ref)
+            return inner
+
+        return lax.fori_loop(0, 2, block_step, carry)
+
+    lax.fori_loop(0, 12, pair_step, 0)
     fit_nodes(acc_ref, frame, out_ref)
-
-
-def fit_call(neighbours, counts, node_place, ext):
+    for buffer, send_sem in ((own_ref, send_own), (halo_ref, send_halo)):
+        view = buffer.at[pl.ds(0, 63)]
+        pltpu.make_async_copy(view, view, send_sem).wait()
+    for k in range(4):
+        pass_copy(k).wait_send()
+    for copy in sib_copies:
+        copy.wait_send()
+
+
+def body(obs_values, obs_place, obs_depth, node_place, neighbours, counts):
     nodes, fan = neighbours.shape
-    tiles = ext.shape[0]
     vmem = pl.BlockSpec(memory_space=pltpu.VMEM)
+    dma = pltpu.SemaphoreType.DMA
     return pl.pallas_call(
-        fit_kernel,
+        full_kernel,
         out_shape=jax.ShapeDtypeStruct((2, 8, nodes), F32),
-        in_specs=[vmem] * 5,
+        in_specs=[vmem] * 6,
         out_specs=vmem,
         scratch_shapes=[
+            pltpu.VMEM((16, 8, LANES), F32),
+            pltpu.VMEM(obs_values.shape, F32),
+            pltpu.VMEM((16, 8, LANES), F32),
+            pltpu.VMEM((64, 24, LANES), F32),
+            pltpu.VMEM((64, 24, LANES), F32),
+            pltpu.VMEM((192, 24, LANES), F32),
             pltpu.VMEM((nodes, fan), F32),
             pltpu.VMEM((nodes, fan), F32),
-            pltpu.VMEM((nodes, tiles, LANES), F32),
+            pltpu.VMEM((nodes, 192, LANES), F32),
             pltpu.VMEM((GROUPS - 1, 8, LANES), F32),
             pltpu.VMEM((GROUPS - 1, 8, LANES), F32),
             pltpu.VMEM((256, 8 * LANES), BF),
             pltpu.VMEM((256, 8 * LANES), BF),
             pltpu.VMEM((256, nodes), F32),
+            dma,
+            dma,
+            dma((12,)),
+            dma((4,)),
+            dma((2,)),
+            dma((2,)),
         ],
-        compiler_params=pltpu.CompilerParams(vmem_limit_bytes=VMEM_LIMIT),
-    )(neighbours, counts.reshape(nodes, 1), node_place, node_place.T, ext)
-
-
-def profile_rows(obs_place, obs_depth):
-    longitude, latitude, day_angle = obs_place[0], obs_place[1], obs_place[2]
-    cos_lat = jnp.cos(latitude)
-    return jnp.stack(
-        [
-            cos_lat * jnp.cos(longitude),
-            cos_lat * jnp.sin(longitude),
-            jnp.sin(latitude),
-            jnp.cos(day_angle),
-            jnp.sin(day_angle),
-            obs_depth.astype(F32),
-            jnp.ones_like(longitude),
-            jnp.zeros_like(longitude),
-        ]
-    )
-
-
-def body(obs_values, obs_place, obs_depth, node_place, neighbours, counts):
-    bands = lax.axis_size("band")
-    tiles = lax.axis_size("tile")
-    levels = obs_values.shape[1] // bands
-    slots = obs_values.shape[2] // tiles
-    values = obs_values.reshape(2, bands, levels, tiles, slots).transpose(1, 3, 0, 2, 4).reshape(bands, tiles, 2 * levels, slots)
-    meta = profile_rows(obs_place, obs_depth).reshape(8, tiles, slots).transpose(1, 0, 2)
-    meta = jnp.broadcast_to(meta[None], (bands,) + meta.shape)
-    rows = jnp.concatenate([values, meta], 2).reshape(bands * tiles, 2 * levels + 8, slots)
-    got = lax.all_to_all(rows, ("band", "tile"), 0, 0, tiled=True)
-    devices = got.shape[0]
-    got = got.reshape(devices // 2, 2, 2 * levels + 8, slots).transpose(0, 2, 1, 3).reshape(devices // 2, 2 * levels + 8, 2 * slots)
-    forward = [(i, (i + 1) % tiles) for i in range(tiles)]
-    backward = [(t, s) for s, t in forward]
-    low = lax.ppermute(got, "tile", forward)
-    high = lax.ppermute(got, "tile", backward)
-    ext = jnp.concatenate([low, got, high], 0)
-    return fit_call(neighbours, counts, node_place, ext)
+        compiler_params=pltpu.CompilerParams(vmem_limit_bytes=VMEM_LIMIT, collective_id=0, has_side_effects=True),
+    )(obs_values, obs_place, obs_depth.reshape(1, -1), node_place, neighbours, counts.reshape(1, nodes))
 
 
 def solution(mesh):

time: 86.8 us -> 47.1 us (0.54)
  blocking collectives: 27.3 us -> 0 us
  Pallas kernels: 31.6 us -> 45 us
  waiting for transfers between devices: 8.21 us -> 0 us
  other arithmetic: 6.56 us -> 0 us
  local copies, waits for them, and re-layouts: 7.59 us -> 1.3 us
  starting transfers between devices: 5.13 us -> 0 us
    all_to_all x1 -> x0, blocking collectives: 27.3 us -> none  [body(): got = lax.all_to_all(rows, ('band', 'tile'), 0, 0, tiled=True)]
    pallas_call x1, Pallas kernels: 31.6 us -> 45 us  [body(): pl.pallas_call(full_kernel, out_shape=jax.ShapeDtypeStruct((2, 8, nodes),...]
    ppermute x2 -> x0, waiting for transfers between devices: 8.21 us -> none  [the longest x1 8.2 us: body(): low = lax.ppermute(got, 'tile', forward)]
    ppermute x2 -> x0, starting transfers between devices: 5.13 us -> none  [the longest x1 5.05 us: body(): high = lax.ppermute(got, 'tile', backward)]
    reshape x4 -> x0, local copies, waits for them, and re-layouts: 3.65 us -> none  [the longest x2 2.07 us: body(): obs_values.reshape(2, bands, levels, tiles, slots).transpose(1, 3, 0, 2, 4)]
    all_to_all x1 -> x0, other arithmetic: 2.51 us -> none  [body(): got = lax.all_to_all(rows, ('band', 'tile'), 0, 0, tiled=True)]
    concatenate x2 -> x0, other arithmetic: 1.67 us -> none  [the longest x1 1.57 us: body(): ext = jnp.concatenate([low, got, high], 0)]
    sin x1 -> x0, other arithmetic: 1.67 us -> none  [profile_rows(): jnp.sin(day_angle)]
  transfers between devices with their start and end apart: 2 -> 0, of which waited for: 1 -> 0; matrix products, arithmetic and copies ran while one was open for 2% -> 0% of each run, Pallas kernels for 0% -> 0%
where the time goes in v2:
time: 47.1 us; the launch traced here: 46.3 us
  Pallas kernels  45 us (96%)
  local copies, waits for them, and re-layouts  1.3 us (3%)
    pallas_call x1, Pallas kernels, body(): pl.pallas_call(full_kernel, out_shape=jax.ShapeDtypeStruct((2, 8, nodes),...  45 us
    unnamed x1, local copies, waits for them, and re-layouts  1.3 us

profile of v2, /device:TPU:0, one launch (start us, length us, event | category | flops | bytes accessed | tf_op | source)
XLA Modules:
  0.0 46.3 jit_solution(12419157720586736783)
XLA Ops:
  0.0 45.0 %shard_map.64 = f32[2,8,128]{2,1,0:T(8,128)} custom-call(f32[2,32,2048]{2,1,0:T(8,128)} %values_ref.1, f32[3,2048]{1,0:T(4,128)} %place_ref.1, s32[1,2048]{1,0:T(1,128)} %bitcast.2, f32[2,128]{1,0:T(2,128)} %node_ref.1, s32[128,1024]{1,0:T(8,128)} %nb_ref.1, s32[1,128]{1,0:T(1,128)} %bitcast.3), custom_call_target="tpu_custom_call" | custom-call | tf_op jit(solution)/shard_map/pallas_call | solution.py:369
  45.0 1.3 %copy.8 = f32[2,8,128]{2,1,0:T(8,128)} copy(f32[2,8,128]{2,1,0:T(8,128)} %shard_map.64) | data formatting | bytes 16384

commit v3 on v2

--- a/solution.py
+++ b/solution.py
@@ -11,6 +11,7 @@
 BF = jnp.bfloat16
 F32 = jnp.float32
 E4 = jnp.float8_e4m3fn
+I8 = jnp.int8
 NT_DIMS = (((1,), (1,)), ((), ()))
 LANES = 128
 MESH = pl.DeviceIdType.MESH
@@ -27,29 +28,33 @@
     slot = chip_slot(lax.shift_right_logical(chip, 4), lax.bitwise_and(lax.shift_right_logical(chip, 2), 3), lax.bitwise_and(chip, 3))
     is_halo = segment == 2 * core
     half = segment - 1 + core
-    hi = slot + jnp.where(is_halo, 128, jnp.where(source_core == core, 0, 64))
+    hi = slot + jnp.where(is_halo, 64, jnp.where(source_core == core, -64, 0))
     lo = jnp.where(is_halo, lax.bitwise_and(nb, 127), lax.bitwise_and(nb, 63) + 64 * half)
-    hi_ref[...] = jnp.where(valid, hi, -1).astype(F32)
-    lo_ref[...] = lo.astype(F32)
+    hi_ref[...] = jnp.where(valid, hi, -128)
+    lo_ref[...] = lo
 
 
 def chip_slot(x, z, y):
     return lax.bitwise_and(x + z + y, 3) * 16 + x * 4 + y
 
 
-def count_node(n, hi_ref, lo_ref, m_ref):
+def count_nodes(step, hi_ref, lo_ref, tmp_ref):
     fan = hi_ref.shape[1]
-    tiles = m_ref.shape[1]
-    hi_ids = lax.broadcasted_iota(jnp.int32, (tiles, fan), 0).astype(BF)
-    lo_ids = lax.broadcasted_iota(jnp.int32, (LANES, fan), 0).astype(BF)
-    hi = jnp.broadcast_to(hi_ref[pl.ds(n, 1), :], (16, fan)).astype(BF)
-    lo = jnp.broadcast_to(lo_ref[pl.ds(n, 1), :], (16, fan)).astype(BF)
-    hi = jnp.concatenate([hi] * (tiles // 16), 0)
-    lo = jnp.concatenate([lo] * (LANES // 16), 0)
-    one, zero = jnp.ones((), BF), jnp.zeros((), BF)
-    hot_hi = jnp.where(hi_ids == hi, one, zero).astype(E4)
-    hot_lo = jnp.where(lo_ids == lo, one, zero).astype(E4)
-    m_ref[pl.ds(n, 1)] = lax.dot_general(hot_hi, hot_lo, NT_DIMS, preferred_element_type=F32)[None]
+    tiles = tmp_ref.shape[1]
+    hi_ids = (lax.broadcasted_iota(jnp.int32, (tiles, fan), 0) - 64).astype(I8)
+    lo_ids = lax.broadcasted_iota(jnp.int32, (LANES, fan), 0).astype(I8)
+    one, zero = jnp.ones((), E4), jnp.zeros((), E4)
+    for i in range(8):
+        n = step * 8 + i
+        hi = jnp.broadcast_to(hi_ref[pl.ds(n, 1), :], (32, fan)).astype(I8)
+        lo = jnp.broadcast_to(lo_ref[pl.ds(n, 1), :], (32, fan)).astype(I8)
+        hot_hi = jnp.where(hi_ids == jnp.concatenate([hi] * (tiles // 32), 0), one, zero)
+        hot_lo = jnp.where(lo_ids == jnp.concatenate([lo] * (LANES // 32), 0), one, zero)
+        tmp_ref[i] = lax.dot_general(hot_hi, hot_lo, NT_DIMS, preferred_element_type=F32)
+
+
+def place_counts(step, tmp_ref, m_ref):
+    m_ref[:, pl.ds(pl.multiple_of(step * 8, 8), 8), :] = jnp.swapaxes(tmp_ref[...], 0, 1)
 
 
 def split2(x):
@@ -90,61 +95,66 @@
     return [x, y, z, c, s, x * x, x * y, x * z, y * y, y * z, x * c, y * c, z * c, x * s, y * s, z * s, c * c, c * s]
 
 
-def ext_block(blk, level_base, ext_ref, m_ref, left, gh_ref, gl_ref, fh_ref, fl_ref, acc_ref):
-    nodes = m_ref.shape[0]
+def build_block(blk, level_base, ext_ref, m_ref, left, gh_ref, gl_ref, fh_ref, fl_ref, w_ref):
+    nodes = m_ref.shape[1]
     start = pl.multiple_of(blk * 8, 8)
     meta = ext_ref[pl.ds(start, 8), 16:24, :]
-    prods = meta_features(meta)
-    for index, prod in enumerate(prods):
+    for index, prod in enumerate(meta_features(meta)):
         high = prod.astype(BF).astype(F32)
         gh_ref[index] = high
         gl_ref[index] = prod - high
-    level = (lax.broadcasted_iota(jnp.int32, (8, LANES), 0) + level_base).astype(F32)
-    zero = jnp.zeros((8, LANES), F32)
-    profile_parts = []
+    row = lax.broadcasted_iota(jnp.int32, (16, LANES), 0)
+    level = (lax.bitwise_and(row, 7) + level_base).astype(F32)
+    level16 = level.astype(BF)
+    zero, one = jnp.zeros((8, LANES), F32), jnp.ones((8, LANES), F32)
+    zero16 = jnp.zeros((16, LANES), BF)
+    parts = []
     for t in range(8):
         cols = pl.ds(t * LANES, LANES)
         rows = ext_ref[start + t]
         tile_meta = rows[16:24]
-        inside = level < jnp.broadcast_to(tile_meta[5:6], (8, LANES))
+        depth = jnp.broadcast_to(tile_meta[5:6], (8, LANES))
+        inside = level[0:8] < depth
+        inside16 = level16 < jnp.concatenate([depth, depth], 0).astype(BF)
         high, mid, low = split3(tile_meta)
         high, mid, low = high.astype(F32), mid.astype(F32), low.astype(F32)
-        profile_parts.append(jnp.concatenate([high, high, high, mid, mid, low], 0).astype(BF))
-        highs = [jnp.where(inside, 1.0, 0.0)]
-        lows = [zero]
-        for index in range(GROUPS - 1):
-            highs.append(jnp.where(inside, jnp.broadcast_to(gh_ref[index, t : t + 1, :], (8, LANES)), zero))
-            lows.append(jnp.where(inside, jnp.broadcast_to(gl_ref[index, t : t + 1, :], (8, LANES)), zero))
+        parts.append(jnp.concatenate([high, high, high, mid, mid, low], 0).astype(BF))
+        for g_ref, f_ref, first in ((gh_ref, fh_ref, one), (gl_ref, fl_ref, zero)):
+            terms = [first] + [jnp.broadcast_to(g_ref[i, t : t + 1, :], (8, LANES)) for i in range(GROUPS - 1)] + [zero]
+            for pair in range(10):
+                both = jnp.concatenate(terms[2 * pair : 2 * pair + 2], 0).astype(BF)
+                f_ref[pl.ds(pair * 16, 16), cols] = jnp.where(inside16, both, zero16)
         factors = [jnp.broadcast_to(tile_meta[i : i + 1], (8, LANES)) for i in range(5)]
         for v in range(2):
             value = jnp.where(inside, rows[8 * v : 8 * v + 8], zero)
-            for term in [value] + [value * factor for factor in factors]:
-                high = term.astype(BF).astype(F32)
-                highs.append(high)
-                lows.append(term - high)
-        highs.append(zero)
-        lows.append(zero)
-        for pair in range(16):
-            part = pl.ds(pair * 16, 16)
-            fh_ref[part, cols] = jnp.concatenate(highs[2 * pair : 2 * pair + 2], 0).astype(BF)
-            fl_ref[part, cols] = jnp.concatenate(lows[2 * pair : 2 * pair + 2], 0).astype(BF)
-    right = jnp.concatenate(profile_parts, 1)
+            terms = [value] + [value * factor for factor in factors]
+            for pair in range(3):
+                both = jnp.concatenate(terms[2 * pair : 2 * pair + 2], 0)
+                high = both.astype(BF)
+                part = pl.ds((10 + 3 * v + pair) * 16, 16)
+                fh_ref[part, cols] = high
+                fl_ref[part, cols] = (both - high.astype(F32)).astype(BF)
+    right = jnp.concatenate(parts, 1)
     power = lax.dot_general(left[:, :48], right, (((1,), (0,)), ((), ())), preferred_element_type=F32)
-    counted = m_ref[:, pl.ds(start, 8), :]
-    counted = jnp.swapaxes(counted.reshape(nodes // 8, 8, 8, LANES), 1, 2)
-    counted = jnp.concatenate([counted[:, t].reshape(nodes, LANES) for t in range(8)], 1)
-    weight = jnp.exp2(power) * counted
-    w_high, w_low = split2(weight)
-    both = jnp.concatenate([w_high, w_low], 0)
-    first = lax.dot_general(fh_ref[...], both, NT_DIMS, preferred_element_type=F32)
-    second = lax.dot_general(fl_ref[...], w_high, NT_DIMS, preferred_element_type=F32)
+    for t in range(8):
+        cols = pl.ds(t * LANES, LANES)
+        w_high, w_low = split2(jnp.exp2(power[:, t * LANES : (t + 1) * LANES]) * m_ref[start + t])
+        w_ref[0:nodes, cols] = w_high
+        w_ref[nodes:, cols] = w_low
+
+
+def add_block(fh_ref, fl_ref, w_ref, acc_ref):
+    nodes = acc_ref.shape[1]
+    first = lax.dot_general(fh_ref[...], w_ref[...], NT_DIMS, preferred_element_type=F32)
+    second = lax.dot_general(fl_ref[...], w_ref[0:nodes, :], NT_DIMS, preferred_element_type=F32)
     acc_ref[...] += first[:, :nodes] + first[:, nodes:] + second
 
 
 def fit_nodes(acc_ref, frame, out_ref):
     nodes = acc_ref.shape[1]
     ex, ey, qx, qy, qz = (jnp.broadcast_to(2.0 * part, (8, nodes)) for part in frame)
-    sums = [acc_ref[8 * i : 8 * i + 8, :] for i in range(GROUPS + 12)]
+    sums = [acc_ref[8 * i : 8 * i + 8, :] for i in range(32)]
+    del sums[GROUPS]
     s1, sx, sy, sz, sc, ss, sxx, sxy, sxz, syy, syz, sxc, syc, szc, sxs, sys_, szs, scc, scs = sums[:GROUPS]
     szz = s1 - sxx - syy
     normal = {
@@ -222,10 +232,60 @@
     return jnp.swapaxes(jnp.stack(rows, 0), 0, 1)
 
 
+def compute(nodes, level_base, before_count, before_pair, left, ext_ref, hi_ref, lo_ref, m_ref, work):
+    tmp_a, tmp_b, gh_a, gl_a, gh_b, gl_b, fh_a, fl_a, w_a, fh_b, fl_b, w_b, acc_ref = work
+    acc_ref[...] = jnp.zeros_like(acc_ref)
+    count_nodes(0, hi_ref, lo_ref, tmp_a)
+    last = nodes // 16 - 1
+
+    def count_step(step, carry):
+        before_count(step)
+        count_nodes(2 * step + 1, hi_ref, lo_ref, tmp_b)
+        place_counts(2 * step, tmp_a, m_ref)
+        count_nodes(2 * step + 2, hi_ref, lo_ref, tmp_a)
+        place_counts(2 * step + 1, tmp_b, m_ref)
+        return carry
+
+    lax.fori_loop(0, last, count_step, 0)
+    before_count(last)
+    count_nodes(2 * last + 1, hi_ref, lo_ref, tmp_b)
+    place_counts(2 * last, tmp_a, m_ref)
+    place_counts(2 * last + 1, tmp_b, m_ref)
+
+    def build(blk, gh_ref, gl_ref, fh_ref, fl_ref, w_ref):
+        build_block(blk, level_base, ext_ref, m_ref, left, gh_ref, gl_ref, fh_ref, fl_ref, w_ref)
+
+    set_a = (gh_a, gl_a, fh_a, fl_a, w_a)
+    set_b = (gh_b, gl_b, fh_b, fl_b, w_b)
+    index = before_pair(0)
+    build(2 * index, *set_a)
+
+    def pair_step(pair, index):
+        following = before_pair(pair + 1)
+        build(2 * index + 1, *set_b)
+        add_block(fh_a, fl_a, w_a, acc_ref)
+        build(2 * following, *set_a)
+        add_block(fh_b, fl_b, w_b, acc_ref)
+        return following
+
+    pairs = ext_ref.shape[0] // 16
+    index = lax.fori_loop(0, pairs - 1, pair_step, index)
+    build(2 * index + 1, *set_b)
+    add_block(fh_a, fl_a, w_a, acc_ref)
+    add_block(fh_b, fl_b, w_b, acc_ref)
+
+
+def work_buffers(nodes):
+    tile = pltpu.VMEM((8, 192, LANES), F32)
+    dense = pltpu.VMEM((GROUPS - 1, 8, LANES), F32)
+    wide = pltpu.VMEM((256, 8 * LANES), BF)
+    return (tile, tile) + (dense,) * 4 + (wide,) * 6 + (pltpu.VMEM((256, nodes), F32),)
+
+
 def full_kernel(
     values_ref, place_ref, depth_ref, node_ref, nb_ref, cnt_ref, out_ref,
     meta_ref, sib_values_ref, sib_meta_ref, own_ref, halo_ref, ext_ref,
-    hi_ref, lo_ref, m_ref, gh_ref, gl_ref, fh_ref, fl_ref, acc_ref,
+    hi_ref, lo_ref, m_ref, work,
     send_own, send_halo, recv, pass_send, sib_send, sib_recv,
 ):
     x = lax.axis_index("band")
@@ -239,9 +299,9 @@
     nodes = nb_ref.shape[0]
 
     def partner(index):
-        dx, dy = lax.rem(lax.div(index, 4), 4), lax.rem(index, 4)
-        dz = lax.rem(lax.div(index, 16) + 8 - dx - dy, 4)
-        other_x, other_z, other_y = lax.rem(x + dx, 4), lax.rem(z + dz, 4), lax.rem(y + dy, 4)
+        dx, dy = lax.bitwise_and(lax.shift_right_logical(index, 2), 3), lax.bitwise_and(index, 3)
+        dz = lax.shift_right_logical(index, 4) + 8 - dx - dy
+        other_x, other_z, other_y = lax.bitwise_and(x + dx, 3), lax.bitwise_and(z + dz, 3), lax.bitwise_and(y + dy, 3)
         pair = other_z * 4 + other_y
         return other_x * 16 + pair, {"band": other_x, "tile": 2 * pair + core}
 
@@ -266,7 +326,6 @@
     columns = packed.T
     left = node_left(columns[:, 0:1], columns[:, 1:2], columns[:, 2:3])
     list_rows(core, nb_ref, columns[:, 3:4], hi_ref, lo_ref)
-    acc_ref[...] = jnp.zeros_like(acc_ref)
 
     pl.semaphore_wait(barrier, 64)
     sib_copies = [
@@ -330,29 +389,18 @@
         wait_group(k)
         pass_copy(k).start()
 
-    def count_step(step, carry):
-        for n in range(8):
-            count_node(step * 8 + n, hi_ref, lo_ref, m_ref)
+    def before_count(step):
         pl.when(step == 1)(send_halos)
-        pl.when((step >= 9) & (lax.rem(step, 2) == 1))(lambda: pass_group(lax.div(step - 9, 2)))
-        return carry
-
-    lax.fori_loop(0, nodes // 8, count_step, 0)
-    level_base = x * 8
-
-    def pair_step(pair, carry):
+        pl.when(step >= 4)(lambda: pass_group(step - 4))
+
+    def before_pair(pair):
         k = lax.rem(phase + 4 - lax.rem(pair, 4), 4)
         index = lax.div(pair, 4) * 4 + k
         pl.when(pair >= 4)(lambda: wait_group(index))
-
-        def block_step(part, inner):
-            ext_block(2 * index + part, level_base, ext_ref, m_ref, left, gh_ref, gl_ref, fh_ref, fl_ref, acc_ref)
-            return inner
-
-        return lax.fori_loop(0, 2, block_step, carry)
-
-    lax.fori_loop(0, 12, pair_step, 0)
-    fit_nodes(acc_ref, frame, out_ref)
+        return index
+
+    compute(nodes, x * 8, before_count, before_pair, left, ext_ref, hi_ref, lo_ref, m_ref, work)
+    fit_nodes(work[-1], frame, out_ref)
     for buffer, send_sem in ((own_ref, send_own), (halo_ref, send_halo)):
         view = buffer.at[pl.ds(0, 63)]
         pltpu.make_async_copy(view, view, send_sem).wait()
@@ -378,14 +426,10 @@
             pltpu.VMEM((64, 24, LANES), F32),
             pltpu.VMEM((64, 24, LANES), F32),
             pltpu.VMEM((192, 24, LANES), F32),
-            pltpu.VMEM((nodes, fan), F32),
-            pltpu.VMEM((nodes, fan), F32),
-            pltpu.VMEM((nodes, 192, LANES), F32),
-            pltpu.VMEM((GROUPS - 1, 8, LANES), F32),
-            pltpu.VMEM((GROUPS - 1, 8, LANES), F32),
-            pltpu.VMEM((256, 8 * LANES), BF),
-            pltpu.VMEM((256, 8 * LANES), BF),
-            pltpu.VMEM((256, nodes), F32),
+            pltpu.VMEM((nodes, fan), jnp.int32),
+            pltpu.VMEM((nodes, fan), jnp.int32),
+            pltpu.VMEM((192, nodes, LANES), F32),
+            work_buffers(nodes),
             dma,
             dma,
             dma((12,)),

time: 47.1 us -> 42.9 us (0.911)
  the two profiles are of different devices: /device:TPU:0 before, /device:TPU:34 now
where the time goes in v3:
time: 42.9 us; the launch traced here: 42.8 us
  Pallas kernels  41.5 us (97%)
  local copies, waits for them, and re-layouts  1.3 us (3%)
    pallas_call x1, Pallas kernels, body(): pl.pallas_call(full_kernel, out_shape=jax.ShapeDtypeStruct((2, 8, nodes),...  41.5 us
    unnamed x1, local copies, waits for them, and re-layouts  1.3 us

profile of v3, /device:TPU:34, one launch (start us, length us, event | category | flops | bytes accessed | tf_op | source)
XLA Modules:
  0.0 42.8 jit_solution(4383599362603766418)
XLA Ops:
  0.0 41.5 %shard_map.64 = f32[2,8,128]{2,1,0:T(8,128)} custom-call(f32[2,32,2048]{2,1,0:T(8,128)} %values_ref.1, f32[3,2048]{1,0:T(4,128)} %place_ref.1, s32[1,2048]{1,0:T(1,128)} %bitcast.2, f32[2,128]{1,0:T(2,128)} %node_ref.1, s32[128,1024]{1,0:T(8,128)} %nb_ref.1, s32[1,128]{1,0:T(1,128)} %bitcast.3), custom_call_target="tpu_custom_call" | custom-call | tf_op jit(solution)/shard_map/pallas_call | solution.py:417
  41.5 1.3 %copy.8 = f32[2,8,128]{2,1,0:T(8,128)} copy(f32[2,8,128]{2,1,0:T(8,128)} %shard_map.64) | data formatting | bytes 16384

commit v4 on v3

--- a/solution.py
+++ b/solution.py
@@ -16,6 +16,7 @@
 LANES = 128
 MESH = pl.DeviceIdType.MESH
 GROUPS = 19
+EARLY = 2
 VMEM_LIMIT = 60 * 2**20
 
 
@@ -38,7 +39,7 @@
     return lax.bitwise_and(x + z + y, 3) * 16 + x * 4 + y
 
 
-def count_nodes(step, hi_ref, lo_ref, tmp_ref):
+def count_nodes(step, hi_ref, lo_ref, tmp_ref, last_ref, m_ref):
     fan = hi_ref.shape[1]
     tiles = tmp_ref.shape[1]
     hi_ids = (lax.broadcasted_iota(jnp.int32, (tiles, fan), 0) - 64).astype(I8)
@@ -51,10 +52,12 @@
         hot_hi = jnp.where(hi_ids == jnp.concatenate([hi] * (tiles // 32), 0), one, zero)
         hot_lo = jnp.where(lo_ids == jnp.concatenate([lo] * (LANES // 32), 0), one, zero)
         tmp_ref[i] = lax.dot_general(hot_hi, hot_lo, NT_DIMS, preferred_element_type=F32)
-
-
-def place_counts(step, tmp_ref, m_ref):
-    m_ref[:, pl.ds(pl.multiple_of(step * 8, 8), 8), :] = jnp.swapaxes(tmp_ref[...], 0, 1)
+        if last_ref is not None:
+            place_counts(step - 1, last_ref, m_ref, i * tiles // 8, (i + 1) * tiles // 8)
+
+
+def place_counts(step, tmp_ref, m_ref, first, stop):
+    m_ref[first:stop, pl.ds(pl.multiple_of(step * 8, 8), 8), :] = jnp.swapaxes(tmp_ref[:, first:stop, :], 0, 1)
 
 
 def split2(x):
@@ -95,35 +98,30 @@
     return [x, y, z, c, s, x * x, x * y, x * z, y * y, y * z, x * c, y * c, z * c, x * s, y * s, z * s, c * c, c * s]
 
 
-def build_block(blk, level_base, ext_ref, m_ref, left, gh_ref, gl_ref, fh_ref, fl_ref, w_ref):
-    nodes = m_ref.shape[1]
+def build_block(blk, level_base, ext_ref, gh_ref, gl_ref, fh_ref, fl_ref):
     start = pl.multiple_of(blk * 8, 8)
     meta = ext_ref[pl.ds(start, 8), 16:24, :]
     for index, prod in enumerate(meta_features(meta)):
         high = prod.astype(BF).astype(F32)
         gh_ref[index] = high
         gl_ref[index] = prod - high
-    row = lax.broadcasted_iota(jnp.int32, (16, LANES), 0)
-    level = (lax.bitwise_and(row, 7) + level_base).astype(F32)
-    level16 = level.astype(BF)
+    level = (lax.broadcasted_iota(jnp.int32, (8, LANES), 0) + level_base).astype(F32)
     zero, one = jnp.zeros((8, LANES), F32), jnp.ones((8, LANES), F32)
-    zero16 = jnp.zeros((16, LANES), BF)
     parts = []
     for t in range(8):
-        cols = pl.ds(t * LANES, LANES)
         rows = ext_ref[start + t]
         tile_meta = rows[16:24]
         depth = jnp.broadcast_to(tile_meta[5:6], (8, LANES))
-        inside = level[0:8] < depth
-        inside16 = level16 < jnp.concatenate([depth, depth], 0).astype(BF)
+        inside = level < depth
+        hold = jnp.where(inside, one, zero)
         high, mid, low = split3(tile_meta)
         high, mid, low = high.astype(F32), mid.astype(F32), low.astype(F32)
         parts.append(jnp.concatenate([high, high, high, mid, mid, low], 0).astype(BF))
-        for g_ref, f_ref, first in ((gh_ref, fh_ref, one), (gl_ref, fl_ref, zero)):
-            terms = [first] + [jnp.broadcast_to(g_ref[i, t : t + 1, :], (8, LANES)) for i in range(GROUPS - 1)] + [zero]
+        for g_ref, f_ref, first in ((gh_ref, fh_ref, hold), (gl_ref, fl_ref, zero)):
+            terms = [jnp.where(inside, jnp.broadcast_to(g_ref[i, t : t + 1, :], (8, LANES)), zero) for i in range(GROUPS - 1)]
+            terms = [first] + terms + [zero]
             for pair in range(10):
-                both = jnp.concatenate(terms[2 * pair : 2 * pair + 2], 0).astype(BF)
-                f_ref[pl.ds(pair * 16, 16), cols] = jnp.where(inside16, both, zero16)
+                f_ref[t, pl.ds(pair * 16, 16)] = jnp.concatenate(terms[2 * pair : 2 * pair + 2], 0).astype(BF)
         factors = [jnp.broadcast_to(tile_meta[i : i + 1], (8, LANES)) for i in range(5)]
         for v in range(2):
             value = jnp.where(inside, rows[8 * v : 8 * v + 8], zero)
@@ -132,28 +130,36 @@
                 both = jnp.concatenate(terms[2 * pair : 2 * pair + 2], 0)
                 high = both.astype(BF)
                 part = pl.ds((10 + 3 * v + pair) * 16, 16)
-                fh_ref[part, cols] = high
-                fl_ref[part, cols] = (both - high.astype(F32)).astype(BF)
-    right = jnp.concatenate(parts, 1)
+                fh_ref[t, part] = high
+                fl_ref[t, part] = (both - high.astype(F32)).astype(BF)
+    return jnp.concatenate(parts, 1)
+
+
+def weigh_block(right, blk, m_ref, left, w_ref):
+    nodes = m_ref.shape[1]
+    start = pl.multiple_of(blk * 8, 8)
     power = lax.dot_general(left[:, :48], right, (((1,), (0,)), ((), ())), preferred_element_type=F32)
     for t in range(8):
-        cols = pl.ds(t * LANES, LANES)
         w_high, w_low = split2(jnp.exp2(power[:, t * LANES : (t + 1) * LANES]) * m_ref[start + t])
-        w_ref[0:nodes, cols] = w_high
-        w_ref[nodes:, cols] = w_low
+        w_ref[t, 0:nodes] = w_high
+        w_ref[t, nodes:] = w_low
 
 
 def add_block(fh_ref, fl_ref, w_ref, acc_ref):
-    nodes = acc_ref.shape[1]
-    first = lax.dot_general(fh_ref[...], w_ref[...], NT_DIMS, preferred_element_type=F32)
-    second = lax.dot_general(fl_ref[...], w_ref[0:nodes, :], NT_DIMS, preferred_element_type=F32)
-    acc_ref[...] += first[:, :nodes] + first[:, nodes:] + second
+    nodes = acc_ref.shape[0]
+    def wide(ref, rows):
+        return jnp.concatenate([ref[t, 0:rows] for t in range(8)], 1)
+
+    first = lax.dot_general(wide(w_ref, 2 * nodes), wide(fh_ref, 256), NT_DIMS, preferred_element_type=F32)
+    second = lax.dot_general(wide(w_ref, nodes), wide(fl_ref, 256), NT_DIMS, preferred_element_type=F32)
+    acc_ref[...] += first[:nodes] + first[nodes:] + second
 
 
 def fit_nodes(acc_ref, frame, out_ref):
-    nodes = acc_ref.shape[1]
+    nodes = acc_ref.shape[0]
+    columns = acc_ref[...].T
     ex, ey, qx, qy, qz = (jnp.broadcast_to(2.0 * part, (8, nodes)) for part in frame)
-    sums = [acc_ref[8 * i : 8 * i + 8, :] for i in range(32)]
+    sums = [columns[8 * i : 8 * i + 8, :] for i in range(32)]
     del sums[GROUPS]
     s1, sx, sy, sz, sc, ss, sxx, sxy, sxz, syy, syz, sxc, syc, szc, sxs, sys_, szs, scc, scs = sums[:GROUPS]
     szz = s1 - sxx - syy
@@ -232,28 +238,31 @@
     return jnp.swapaxes(jnp.stack(rows, 0), 0, 1)
 
 
-def compute(nodes, level_base, before_count, before_pair, left, ext_ref, hi_ref, lo_ref, m_ref, work):
+def compute(nodes, level_base, early, start, before_count, before_pair, left, ext_ref, hi_ref, lo_ref, m_ref, work):
     tmp_a, tmp_b, gh_a, gl_a, gh_b, gl_b, fh_a, fl_a, w_a, fh_b, fl_b, w_b, acc_ref = work
     acc_ref[...] = jnp.zeros_like(acc_ref)
-    count_nodes(0, hi_ref, lo_ref, tmp_a)
+    count_nodes(0, hi_ref, lo_ref, tmp_a, None, None)
     last = nodes // 16 - 1
+
+    def count_pair(step, carry):
+        count_nodes(2 * step + 1, hi_ref, lo_ref, tmp_b, tmp_a, m_ref)
+        count_nodes(2 * step + 2, hi_ref, lo_ref, tmp_a, tmp_b, m_ref)
+        return carry
 
     def count_step(step, carry):
         before_count(step)
-        count_nodes(2 * step + 1, hi_ref, lo_ref, tmp_b)
-        place_counts(2 * step, tmp_a, m_ref)
-        count_nodes(2 * step + 2, hi_ref, lo_ref, tmp_a)
-        place_counts(2 * step + 1, tmp_b, m_ref)
-        return carry
-
-    lax.fori_loop(0, last, count_step, 0)
+        return count_pair(step, carry)
+
+    lax.fori_loop(0, early, count_pair, 0)
+    start()
+    lax.fori_loop(early, last, count_step, 0)
     before_count(last)
-    count_nodes(2 * last + 1, hi_ref, lo_ref, tmp_b)
-    place_counts(2 * last, tmp_a, m_ref)
-    place_counts(2 * last + 1, tmp_b, m_ref)
+    count_nodes(2 * last + 1, hi_ref, lo_ref, tmp_b, tmp_a, m_ref)
+    place_counts(2 * last + 1, tmp_b, m_ref, 0, m_ref.shape[0])
 
     def build(blk, gh_ref, gl_ref, fh_ref, fl_ref, w_ref):
-        build_block(blk, level_base, ext_ref, m_ref, left, gh_ref, gl_ref, fh_ref, fl_ref, w_ref)
+        right = build_block(blk, level_base, ext_ref, gh_ref, gl_ref, fh_ref, fl_ref)
+        weigh_block(right, blk, m_ref, left, w_ref)
 
     set_a = (gh_a, gl_a, fh_a, fl_a, w_a)
     set_b = (gh_b, gl_b, fh_b, fl_b, w_b)
@@ -278,8 +287,8 @@
 def work_buffers(nodes):
     tile = pltpu.VMEM((8, 192, LANES), F32)
     dense = pltpu.VMEM((GROUPS - 1, 8, LANES), F32)
-    wide = pltpu.VMEM((256, 8 * LANES), BF)
-    return (tile, tile) + (dense,) * 4 + (wide,) * 6 + (pltpu.VMEM((256, nodes), F32),)
+    wide = pltpu.VMEM((8, 256, LANES), BF)
+    return (tile, tile) + (dense,) * 4 + (wide,) * 6 + (pltpu.VMEM((nodes, 256), F32),)
 
 
 def full_kernel(
@@ -327,13 +336,10 @@
     left = node_left(columns[:, 0:1], columns[:, 1:2], columns[:, 2:3])
     list_rows(core, nb_ref, columns[:, 3:4], hi_ref, lo_ref)
 
-    pl.semaphore_wait(barrier, 64)
     sib_copies = [
         pltpu.make_async_remote_copy(values_ref, sib_values_ref, sib_send.at[0], sib_recv.at[0], device_id=sibling, device_id_type=MESH),
         pltpu.make_async_remote_copy(meta_ref, sib_meta_ref, sib_send.at[1], sib_recv.at[1], device_id=sibling, device_id_type=MESH),
     ]
-    for copy in sib_copies:
-        copy.start()
 
     def send(buffer, base, send_sem):
         def step(index, carry):
@@ -354,8 +360,12 @@
     def wait_group(index):
         pltpu.make_async_copy(group(index), group(index), recv.at[index]).wait()
 
-    keep(own_ref, 0).start()
-    send(own_ref, 0, send_own)
+    def start():
+        pl.semaphore_wait(barrier, 64)
+        for copy in sib_copies:
+            copy.start()
+        keep(own_ref, 0).start()
+        send(own_ref, 0, send_own)
 
     def send_halos():
         for copy in sib_copies:
@@ -384,22 +394,17 @@
             group(k), group(4 + k), pass_send.at[k], recv.at[4 + k], device_id=sibling, device_id_type=MESH
         )
 
-    def pass_group(order):
-        k = lax.rem(phase + 4 - order, 4)
-        wait_group(k)
-        pass_copy(k).start()
-
     def before_count(step):
-        pl.when(step == 1)(send_halos)
-        pl.when(step >= 4)(lambda: pass_group(step - 4))
+        pl.when(step == EARLY + 1)(send_halos)
 
     def before_pair(pair):
-        k = lax.rem(phase + 4 - lax.rem(pair, 4), 4)
-        index = lax.div(pair, 4) * 4 + k
-        pl.when(pair >= 4)(lambda: wait_group(index))
+        k = lax.bitwise_and(phase + 4 - pair, 3)
+        index = pair - lax.bitwise_and(pair, 3) + k
+        wait_group(index)
+        pl.when(pair < 4)(lambda: pass_copy(k).start())
         return index
 
-    compute(nodes, x * 8, before_count, before_pair, left, ext_ref, hi_ref, lo_ref, m_ref, work)
+    compute(nodes, x * 8, EARLY, start, before_count, before_pair, left, ext_ref, hi_ref, lo_ref, m_ref, work)
     fit_nodes(work[-1], frame, out_ref)
     for buffer, send_sem in ((own_ref, send_own), (halo_ref, send_halo)):
         view = buffer.at[pl.ds(0, 63)]

time: 42.9 us -> 38.2 us (0.89)
  the two profiles are of different devices: /device:TPU:34 before, /device:TPU:26 now
where the time goes in v4:
time: 38.2 us; the launch traced here: 38 us
  Pallas kernels  36.7 us (96%)
  local copies, waits for them, and re-layouts  1.3 us (3%)
    pallas_call x1, Pallas kernels, body(): pl.pallas_call(full_kernel, out_shape=jax.ShapeDtypeStruct((2, 8, nodes),...  36.7 us
    unnamed x1, local copies, waits for them, and re-layouts  1.3 us

profile of v4, /device:TPU:26, one launch (start us, length us, event | category | flops | bytes accessed | tf_op | source)
XLA Modules:
  0.0 38.0 jit_solution(11962569876501061588)
XLA Ops:
  0.0 36.7 %shard_map.64 = f32[2,8,128]{2,1,0:T(8,128)} custom-call(f32[2,32,2048]{2,1,0:T(8,128)} %values_ref.1, f32[3,2048]{1,0:T(4,128)} %place_ref.1, s32[1,2048]{1,0:T(1,128)} %bitcast.2, f32[2,128]{1,0:T(2,128)} %node_ref.1, s32[128,1024]{1,0:T(8,128)} %nb_ref.1, s32[1,128]{1,0:T(1,128)} %bitcast.3), custom_call_target="tpu_custom_call" | custom-call | tf_op jit(solution)/shard_map/pallas_call | solution.py:422
  36.7 1.3 %copy.8 = f32[2,8,128]{2,1,0:T(8,128)} copy(f32[2,8,128]{2,1,0:T(8,128)} %shard_map.64) | data formatting | bytes 16384

commit v5 on v4

--- a/solution.py
+++ b/solution.py
@@ -16,7 +16,8 @@
 LANES = 128
 MESH = pl.DeviceIdType.MESH
 GROUPS = 19
-EARLY = 2
+EARLY = 1
+ROWS = 21
 VMEM_LIMIT = 60 * 2**20
 
 
@@ -79,7 +80,7 @@
     vals = jnp.where(
         row == 0,
         node_x * scale,
-        jnp.where(row == 1, node_y * scale, jnp.where(row == 2, node_z * scale, jnp.where(row == 6, -scale, 0.0))),
+        jnp.where(row == 1, node_y * scale, jnp.where(row == 2, node_z * scale, jnp.where(row == 3, -scale, 0.0))),
     )
     high, mid, low = split3(vals)
     block = lax.shift_right_logical(col, 3)
@@ -94,14 +95,21 @@
 
 def meta_features(meta):
     dense = jnp.swapaxes(meta, 0, 1)
-    x, y, z, c, s = (dense[i] for i in range(5))
-    return [x, y, z, c, s, x * x, x * y, x * z, y * y, y * z, x * c, y * c, z * c, x * s, y * s, z * s, c * c, c * s]
+    y, z, c, s = (dense[i] for i in range(4))
+    x = jnp.sqrt(jnp.maximum(1.0 - y * y - z * z, 0.0))
+    one, zero = jnp.ones_like(x), jnp.zeros_like(x)
+    rows = jnp.swapaxes(jnp.stack([x, y, z, one, c, s, zero, zero], 0), 0, 1)
+    products = [x, y, z, c, s, x * x, x * y, x * z, y * y, y * z, x * c, y * c, z * c, x * s, y * s, z * s, c * c, c * s]
+    return products, rows
 
 
 def build_block(blk, level_base, ext_ref, gh_ref, gl_ref, fh_ref, fl_ref):
     start = pl.multiple_of(blk * 8, 8)
     meta = ext_ref[pl.ds(start, 8), 16:24, :]
-    for index, prod in enumerate(meta_features(meta)):
+    products, features = meta_features(meta)
+    for t in range(8):
+        gh_ref[GROUPS - 1 + t] = features[t]
+    for index, prod in enumerate(products):
         high = prod.astype(BF).astype(F32)
         gh_ref[index] = high
         gl_ref[index] = prod - high
@@ -110,11 +118,10 @@
     parts = []
     for t in range(8):
         rows = ext_ref[start + t]
-        tile_meta = rows[16:24]
-        depth = jnp.broadcast_to(tile_meta[5:6], (8, LANES))
+        depth = jnp.broadcast_to(rows[20:21], (8, LANES))
         inside = level < depth
         hold = jnp.where(inside, one, zero)
-        high, mid, low = split3(tile_meta)
+        high, mid, low = split3(features[t])
         high, mid, low = high.astype(F32), mid.astype(F32), low.astype(F32)
         parts.append(jnp.concatenate([high, high, high, mid, mid, low], 0).astype(BF))
         for g_ref, f_ref, first in ((gh_ref, fh_ref, hold), (gl_ref, fl_ref, zero)):
@@ -122,7 +129,7 @@
             terms = [first] + terms + [zero]
             for pair in range(10):
                 f_ref[t, pl.ds(pair * 16, 16)] = jnp.concatenate(terms[2 * pair : 2 * pair + 2], 0).astype(BF)
-        factors = [jnp.broadcast_to(tile_meta[i : i + 1], (8, LANES)) for i in range(5)]
+        factors = [jnp.broadcast_to(gh_ref[GROUPS - 1 + t, i : i + 1, :], (8, LANES)) for i in (0, 1, 2, 4, 5)]
         for v in range(2):
             value = jnp.where(inside, rows[8 * v : 8 * v + 8], zero)
             terms = [value] + [value * factor for factor in factors]
@@ -224,15 +231,17 @@
 
 def profile_meta(place_ref, depth_ref):
     longitude, latitude, day_angle = (dense_rows(place_ref, row) for row in range(3))
+    pair = lax.broadcasted_iota(jnp.int32, longitude.shape, 0).astype(F32)
+    longitude = longitude - (pair * (math.pi / 8) + (math.pi / 16 - math.pi))
     cos_lat = jnp.cos(latitude)
     rows = [
-        cos_lat * jnp.cos(longitude),
         cos_lat * jnp.sin(longitude),
         jnp.sin(latitude),
         jnp.cos(day_angle),
         jnp.sin(day_angle),
         dense_rows(depth_ref, 0).astype(F32),
-        jnp.ones_like(cos_lat),
+        cos_lat * jnp.cos(longitude),
+        jnp.zeros_like(cos_lat),
         jnp.zeros_like(cos_lat),
     ]
     return jnp.swapaxes(jnp.stack(rows, 0), 0, 1)
@@ -286,7 +295,7 @@
 
 def work_buffers(nodes):
     tile = pltpu.VMEM((8, 192, LANES), F32)
-    dense = pltpu.VMEM((GROUPS - 1, 8, LANES), F32)
+    dense = pltpu.VMEM((GROUPS + 7, 8, LANES), F32)
     wide = pltpu.VMEM((8, 256, LANES), BF)
     return (tile, tile) + (dense,) * 4 + (wide,) * 6 + (pltpu.VMEM((nodes, 256), F32),)
 
@@ -330,7 +339,8 @@
             for v in range(2):
                 own_ref[b * 16 + m, 8 * v : 8 * v + 8, :] = values_ref[v, 8 * b : 8 * b + 8, m * LANES : (m + 1) * LANES]
             own_ref[b * 16 + m, 16:24, :] = meta_ref[m]
-    point, frame = node_frame(node_ref[0:1, :], node_ref[1:2, :])
+    middle = jnp.full((1, nodes), chip, jnp.int32).astype(F32) * (math.pi / 8) + (math.pi / 16 - math.pi)
+    point, frame = node_frame(node_ref[0:1, :] - middle, node_ref[1:2, :])
     packed = jnp.concatenate(list(point) + [cnt_ref[...].astype(F32)] + [jnp.zeros((124, nodes), F32)], 0)
     columns = packed.T
     left = node_left(columns[:, 0:1], columns[:, 1:2], columns[:, 2:3])
@@ -345,17 +355,17 @@
         def step(index, carry):
             unit, device = partner(index)
             pltpu.make_async_remote_copy(
-                buffer.at[unit], ext_ref.at[16 * base + mine], send_sem, recv.at[base + phase], device_id=device, device_id_type=MESH
+                buffer.at[unit, pl.ds(0, ROWS)], ext_ref.at[16 * base + mine, pl.ds(0, ROWS)], send_sem, recv.at[base + phase], device_id=device, device_id_type=MESH
             ).start()
             return carry
 
         lax.fori_loop(1, 64, step, 0)
 
     def keep(buffer, base):
-        return pltpu.make_async_copy(buffer.at[x * 16 + chip], ext_ref.at[16 * base + mine], recv.at[base + phase])
+        return pltpu.make_async_copy(buffer.at[x * 16 + chip, pl.ds(0, ROWS)], ext_ref.at[16 * base + mine, pl.ds(0, ROWS)], recv.at[base + phase])
 
     def group(index):
-        return ext_ref.at[pl.ds(pl.multiple_of(index * 16, 16), 16)]
+        return ext_ref.at[pl.ds(pl.multiple_of(index * 16, 16), 16), pl.ds(0, ROWS)]
 
     def wait_group(index):
         pltpu.make_async_copy(group(index), group(index), recv.at[index]).wait()
@@ -370,12 +380,16 @@
     def send_halos():
         for copy in sib_copies:
             copy.wait_recv()
+        turn = jnp.full((1, LANES), 2 * core - 1, jnp.int32).astype(F32) * math.sin(math.pi / 8)
+        first_row = lax.broadcasted_iota(jnp.int32, (8, LANES), 0) == 0
         from_own = lax.shift_right_logical(lax.broadcasted_iota(jnp.int32, (8, LANES), 1), 6) == core
 
         def step(m, carry):
             other = lax.rem(m + 15 + 2 * core, 16)
             cols = pl.ds(pl.multiple_of(other * LANES, LANES), LANES)
             meta = jnp.where(from_own, pltpu.roll(meta_ref[other], 64, 1), sib_meta_ref[other])
+            turned = meta[0:1] * math.cos(math.pi / 8) + meta[5:6] * turn
+            meta = jnp.where(first_row, jnp.broadcast_to(turned, (8, LANES)), meta)
             for b in range(4):
                 unit = b * 16 + m
                 for v in range(2):
@@ -407,7 +421,7 @@
     compute(nodes, x * 8, EARLY, start, before_count, before_pair, left, ext_ref, hi_ref, lo_ref, m_ref, work)
     fit_nodes(work[-1], frame, out_ref)
     for buffer, send_sem in ((own_ref, send_own), (halo_ref, send_halo)):
-        view = buffer.at[pl.ds(0, 63)]
+        view = buffer.at[pl.ds(0, 63), pl.ds(0, ROWS)]
         pltpu.make_async_copy(view, view, send_sem).wait()
     for k in range(4):
         pass_copy(k).wait_send()

time: 38.2 us -> 37.7 us (0.987)
  the two profiles are of different devices: /device:TPU:26 before, /device:TPU:1 now
where the time goes in v5:
time: 37.7 us; the launch traced here: 37.5 us
  Pallas kernels  36.2 us (96%)
  local copies, waits for them, and re-layouts  1.3 us (3%)
    pallas_call x1, Pallas kernels, body(): pl.pallas_call(full_kernel, out_shape=jax.ShapeDtypeStruct((2, 8, nodes),...  36.2 us
    unnamed x1, local copies, waits for them, and re-layouts  1.3 us

profile of v5, /device:TPU:1, one launch (start us, length us, event | category | flops | bytes accessed | tf_op | source)
XLA Modules:
  0.0 37.5 jit_solution(18047047754785473018)
XLA Ops:
  0.0 36.2 %shard_map.64 = f32[2,8,128]{2,1,0:T(8,128)} custom-call(f32[2,32,2048]{2,1,0:T(8,128)} %values_ref.1, f32[3,2048]{1,0:T(4,128)} %place_ref.1, s32[1,2048]{1,0:T(1,128)} %bitcast.2, f32[2,128]{1,0:T(2,128)} %node_ref.1, s32[128,1024]{1,0:T(8,128)} %nb_ref.1, s32[1,128]{1,0:T(1,128)} %bitcast.3), custom_call_target="tpu_custom_call" | custom-call | tf_op jit(solution)/shard_map/pallas_call | solution.py:436
  36.2 1.3 %copy.8 = f32[2,8,128]{2,1,0:T(8,128)} copy(f32[2,8,128]{2,1,0:T(8,128)} %shard_map.64) | data formatting | bytes 16384

commit v6 on v5

--- a/solution.py
+++ b/solution.py
@@ -251,23 +251,27 @@
     tmp_a, tmp_b, gh_a, gl_a, gh_b, gl_b, fh_a, fl_a, w_a, fh_b, fl_b, w_b, acc_ref = work
     acc_ref[...] = jnp.zeros_like(acc_ref)
     count_nodes(0, hi_ref, lo_ref, tmp_a, None, None)
-    last = nodes // 16 - 1
-
-    def count_pair(step, carry):
-        count_nodes(2 * step + 1, hi_ref, lo_ref, tmp_b, tmp_a, m_ref)
-        count_nodes(2 * step + 2, hi_ref, lo_ref, tmp_a, tmp_b, m_ref)
+
+    def count_group(step, odd):
+        now, last = (tmp_b, tmp_a) if odd else (tmp_a, tmp_b)
+        count_nodes(step, hi_ref, lo_ref, now, last, m_ref)
+
+    def count_four(step, carry):
+        for i in range(4):
+            count_group(4 * step + 1 + i, i % 2 == 0)
         return carry
 
     def count_step(step, carry):
         before_count(step)
-        return count_pair(step, carry)
-
-    lax.fori_loop(0, early, count_pair, 0)
+        return count_four(step, carry)
+
+    rounds = (nodes // 8 - 1) // 4
+    lax.fori_loop(0, early, count_four, 0)
     start()
-    lax.fori_loop(early, last, count_step, 0)
-    before_count(last)
-    count_nodes(2 * last + 1, hi_ref, lo_ref, tmp_b, tmp_a, m_ref)
-    place_counts(2 * last + 1, tmp_b, m_ref, 0, m_ref.shape[0])
+    lax.fori_loop(early, rounds, count_step, 0)
+    for step in range(4 * rounds + 1, nodes // 8):
+        count_group(step, step % 2 == 1)
+    place_counts(nodes // 8 - 1, tmp_b, m_ref, 0, m_ref.shape[0])
 
     def build(blk, gh_ref, gl_ref, fh_ref, fl_ref, w_ref):
         right = build_block(blk, level_base, ext_ref, gh_ref, gl_ref, fh_ref, fl_ref)

time: 37.7 us -> 37.1 us (0.984)
  the two profiles are of different devices: /device:TPU:1 before, /device:TPU:96 now
where the time goes in v6:
time: 37.1 us; the launch traced here: 36.9 us
  Pallas kernels  35.6 us (96%)
  local copies, waits for them, and re-layouts  1.3 us (4%)
    pallas_call x1, Pallas kernels, body(): pl.pallas_call(full_kernel, out_shape=jax.ShapeDtypeStruct((2, 8, nodes),...  35.6 us
    unnamed x1, local copies, waits for them, and re-layouts  1.3 us

profile of v6, /device:TPU:96, one launch (start us, length us, event | category | flops | bytes accessed | tf_op | source)
XLA Modules:
  0.0 36.9 jit_solution(8103141041407895544)
XLA Ops:
  0.0 35.6 %shard_map.64 = f32[2,8,128]{2,1,0:T(8,128)} custom-call(f32[2,32,2048]{2,1,0:T(8,128)} %values_ref.1, f32[3,2048]{1,0:T(4,128)} %place_ref.1, s32[1,2048]{1,0:T(1,128)} %bitcast.2, f32[2,128]{1,0:T(2,128)} %node_ref.1, s32[128,1024]{1,0:T(8,128)} %nb_ref.1, s32[1,128]{1,0:T(1,128)} %bitcast.3), custom_call_target="tpu_custom_call" | custom-call | tf_op jit(solution)/shard_map/pallas_call | solution.py:440
  35.6 1.3 %copy.8 = f32[2,8,128]{2,1,0:T(8,128)} copy(f32[2,8,128]{2,1,0:T(8,128)} %shard_map.64) | data formatting | bytes 16384

commit v7 on v6

--- a/solution.py
+++ b/solution.py
@@ -16,7 +16,7 @@
 LANES = 128
 MESH = pl.DeviceIdType.MESH
 GROUPS = 19
-EARLY = 1
+EARLY = 4
 ROWS = 21
 VMEM_LIMIT = 60 * 2**20
 
@@ -250,26 +250,24 @@
 def compute(nodes, level_base, early, start, before_count, before_pair, left, ext_ref, hi_ref, lo_ref, m_ref, work):
     tmp_a, tmp_b, gh_a, gl_a, gh_b, gl_b, fh_a, fl_a, w_a, fh_b, fl_b, w_b, acc_ref = work
     acc_ref[...] = jnp.zeros_like(acc_ref)
-    count_nodes(0, hi_ref, lo_ref, tmp_a, None, None)
-
     def count_group(step, odd):
         now, last = (tmp_b, tmp_a) if odd else (tmp_a, tmp_b)
         count_nodes(step, hi_ref, lo_ref, now, last, m_ref)
 
-    def count_four(step, carry):
-        for i in range(4):
-            count_group(4 * step + 1 + i, i % 2 == 0)
-        return carry
+    count_nodes(0, hi_ref, lo_ref, tmp_a, None, None)
+    for step in range(1, early):
+        count_group(step, step % 2 == 1)
+    start()
 
     def count_step(step, carry):
         before_count(step)
-        return count_four(step, carry)
-
-    rounds = (nodes // 8 - 1) // 4
-    lax.fori_loop(0, early, count_four, 0)
-    start()
-    lax.fori_loop(early, rounds, count_step, 0)
-    for step in range(4 * rounds + 1, nodes // 8):
+        for i in range(4):
+            count_group(early + 4 * step + i, (early + i) % 2 == 1)
+        return carry
+
+    rounds = (nodes // 8 - early) // 4
+    lax.fori_loop(0, rounds, count_step, 0)
+    for step in range(early + 4 * rounds, nodes // 8):
         count_group(step, step % 2 == 1)
     place_counts(nodes // 8 - 1, tmp_b, m_ref, 0, m_ref.shape[0])
 
@@ -305,10 +303,11 @@
 
 
 def full_kernel(
-    values_ref, place_ref, depth_ref, node_ref, nb_ref, cnt_ref, out_ref,
+    values_hbm, place_ref, depth_ref, node_ref, nb_hbm, cnt_ref, out_ref,
+    values_ref, nb_ref,
     meta_ref, sib_values_ref, sib_meta_ref, own_ref, halo_ref, ext_ref,
     hi_ref, lo_ref, m_ref, work,
-    send_own, send_halo, recv, pass_send, sib_send, sib_recv,
+    send_own, send_halo, recv, pass_send, sib_send, sib_recv, load_sem,
 ):
     x = lax.axis_index("band")
     tile = lax.axis_index("tile")
@@ -327,17 +326,24 @@
         pair = other_z * 4 + other_y
         return other_x * 16 + pair, {"band": other_x, "tile": 2 * pair + core}
 
+    loads = [
+        pltpu.make_async_copy(values_hbm, values_ref, load_sem.at[0]),
+        pltpu.make_async_copy(nb_hbm, nb_ref, load_sem.at[1]),
+    ]
+    for load in loads:
+        load.start()
     barrier = pltpu.get_barrier_semaphore()
 
     def greet(index, carry):
-        _, device = partner(index)
+        _, device = partner(index + 1)
         pl.semaphore_signal(barrier, inc=1, device_id=device, device_id_type=MESH)
         return carry
 
-    lax.fori_loop(1, 64, greet, 0)
+    lax.fori_loop(0, 63, greet, 0, unroll=7)
     pl.semaphore_signal(barrier, inc=1, device_id=sibling, device_id_type=MESH)
 
     meta_ref[...] = profile_meta(place_ref, depth_ref)
+    loads[0].wait()
     for b in range(4):
         for m in range(16):
             for v in range(2):
@@ -348,6 +354,7 @@
     packed = jnp.concatenate(list(point) + [cnt_ref[...].astype(F32)] + [jnp.zeros((124, nodes), F32)], 0)
     columns = packed.T
     left = node_left(columns[:, 0:1], columns[:, 1:2], columns[:, 2:3])
+    loads[1].wait()
     list_rows(core, nb_ref, columns[:, 3:4], hi_ref, lo_ref)
 
     sib_copies = [
@@ -357,13 +364,13 @@
 
     def send(buffer, base, send_sem):
         def step(index, carry):
-            unit, device = partner(index)
+            unit, device = partner(index + 1)
             pltpu.make_async_remote_copy(
                 buffer.at[unit, pl.ds(0, ROWS)], ext_ref.at[16 * base + mine, pl.ds(0, ROWS)], send_sem, recv.at[base + phase], device_id=device, device_id_type=MESH
             ).start()
             return carry
 
-        lax.fori_loop(1, 64, step, 0)
+        lax.fori_loop(0, 63, step, 0, unroll=7)
 
     def keep(buffer, base):
         return pltpu.make_async_copy(buffer.at[x * 16 + chip, pl.ds(0, ROWS)], ext_ref.at[16 * base + mine, pl.ds(0, ROWS)], recv.at[base + phase])
@@ -413,7 +420,7 @@
         )
 
     def before_count(step):
-        pl.when(step == EARLY + 1)(send_halos)
+        pl.when(step == 1)(send_halos)
 
     def before_pair(pair):
         k = lax.bitwise_and(phase + 4 - pair, 3)
@@ -436,13 +443,16 @@
 def body(obs_values, obs_place, obs_depth, node_place, neighbours, counts):
     nodes, fan = neighbours.shape
     vmem = pl.BlockSpec(memory_space=pltpu.VMEM)
+    hbm = pl.BlockSpec(memory_space=pl.ANY)
     dma = pltpu.SemaphoreType.DMA
     return pl.pallas_call(
         full_kernel,
         out_shape=jax.ShapeDtypeStruct((2, 8, nodes), F32),
-        in_specs=[vmem] * 6,
+        in_specs=[hbm, vmem, vmem, vmem, hbm, vmem],
         out_specs=vmem,
         scratch_shapes=[
+            pltpu.VMEM(obs_values.shape, F32),
+            pltpu.VMEM((nodes, fan), jnp.int32),
             pltpu.VMEM((16, 8, LANES), F32),
             pltpu.VMEM(obs_values.shape, F32),
             pltpu.VMEM((16, 8, LANES), F32),
@@ -459,6 +469,7 @@
             dma((4,)),
             dma((2,)),
             dma((2,)),
+            dma((2,)),
         ],
         compiler_params=pltpu.CompilerParams(vmem_limit_bytes=VMEM_LIMIT, collective_id=0, has_side_effects=True),
     )(obs_values, obs_place, obs_depth.reshape(1, -1), node_place, neighbours, counts.reshape(1, nodes))

time: 37.1 us -> 35.8 us (0.965)
  the two profiles are of different devices: /device:TPU:96 before, /device:TPU:0 now
where the time goes in v7:
time: 35.8 us; the launch traced here: 35.2 us
  Pallas kernels  33.9 us (95%)
  local copies, waits for them, and re-layouts  1.3 us (4%)
    pallas_call x1, Pallas kernels, body(): pl.pallas_call(full_kernel, out_shape=jax.ShapeDtypeStruct((2, 8, nodes),...  33.9 us
    unnamed x1, local copies, waits for them, and re-layouts  1.3 us

profile of v7, /device:TPU:0, one launch (start us, length us, event | category | flops | bytes accessed | tf_op | source)
XLA Modules:
  0.0 35.2 jit_solution(821211357739785923)
XLA Ops:
  0.0 33.9 %shard_map.64 = f32[2,8,128]{2,1,0:T(8,128)} custom-call(f32[2,32,2048]{2,1,0:T(8,128)} %values_hbm.1, f32[3,2048]{1,0:T(4,128)} %place_ref.1, s32[1,2048]{1,0:T(1,128)} %bitcast.2, f32[2,128]{1,0:T(2,128)} %node_ref.1, s32[128,1024]{1,0:T(8,128)} %nb_hbm.1, s32[1,128]{1,0:T(1,128)} %bitcast.3), custom_call_target="tpu_custom_call" | custom-call | tf_op jit(solution)/shard_map/pallas_call | solution.py:448
  33.9 1.3 %copy.8 = f32[2,8,128]{2,1,0:T(8,128)} copy(f32[2,8,128]{2,1,0:T(8,128)} %shard_map.64) | data formatting | bytes 16384
